TPU v7x, 32 devices: a whole 2x2x4 slice. The times are simulated.
32 devices in a mesh: star: 8 (over y, x, core), row: 4 (over z).
Axes of the slice: x: 2, y: 2, z: 4, core: 2. Of those that a mesh axis runs over, the one named last changes fastest.
Arguments:
- feature_maps: bfloat16 [64, 1024, 1024], P(None, 'row'), may hold values from -6 to 6
- coef_table: bfloat16 [64, 64], replicated, may hold values from -0.119628906 to 0.119628906
- star_counts: int32 [8], replicated, may hold values from 1 to 12, 32 in all
- star_cells: int32 [8, 12], replicated, may hold values from 0 to 63
- star_bands: int32 [8, 12], replicated, may hold values from 0 to 7
- psf_cotangent: bfloat16 [96, 1024, 1024], P('star', 'row'), may hold values from -6 to 6
Outputs:
- map_grad: float32 [64, 1024, 1024], P('star', 'row')
- coef_grad: float32 [64, 64], replicated
Inputs may be any that keep to these rules, and one draw needn't show every extreme that they name: The live stars of group g fill its slots 0 to star_counts[g] - 1; the counts sum to 32, and some group has exactly 12.
All inputs are finite; a program needn't handle non-finite values.
Results may differ from a plain program's by a relative error of at most 0.008.
Values may be sent and summed in bfloat16 or wider, within the bound.
A program may use at most 192 MiB of HBM per device.

v0:
```python
import functools

import jax
import jax.numpy as jnp
import numpy as np
from jax import lax
from jax.experimental import pallas as pl
from jax.experimental.pallas import tpu as pltpu
from jax.sharding import PartitionSpec as P

BANDS = 8
LIVE_DEV = 4
PLANE_DEV = 8
RADIX = 4
ROWS_STEP = 16
F32 = jnp.float32
BF16 = jnp.bfloat16


def fourier_tables(pupil_size):
    index_row = jnp.arange(pupil_size, dtype=jnp.int32)
    products = index_row[:, None] * index_row[None, :] % pupil_size
    angles = 2.0 * jnp.pi / pupil_size * products.astype(jnp.float32)
    return (jnp.cos(angles).astype(jnp.bfloat16), (-jnp.sin(angles)).astype(jnp.bfloat16))


def aperture_rows(first_row, row_count, pupil_size):
    centre = 0.5 * (pupil_size - 1)
    row_pos = (first_row + jnp.arange(row_count, dtype=jnp.int32)).astype(jnp.float32) - centre
    col_pos = jnp.arange(pupil_size, dtype=jnp.int32).astype(jnp.float32) - centre
    radius = row_pos[:, None] * row_pos[:, None] + col_pos[None, :] * col_pos[None, :]
    return jnp.where(radius <= 0.25 * pupil_size * pupil_size, 1.0, 0.0).astype(jnp.float32)


def wave_numbers(band_ids):
    wavelength = 0.55 + 0.35 * band_ids.astype(jnp.float32) / (BANDS - 1)
    return 2.0 * jnp.pi / wavelength


def table_pick(values, indices):
    positions = jnp.arange(values.shape[0], dtype=jnp.int32)
    chosen = jnp.where(positions[None, :] == indices[:, None], values[None, :], 0)
    return jnp.sum(chosen, axis=1)


def per_device(feature_maps, coef_table, star_counts, star_cells, star_bands, psf_cotangent):
    groups = lax.axis_size("star")
    my_group = lax.axis_index("star")
    slot_count = psf_cotangent.shape[0]
    map_count, row_count, pupil_size = feature_maps.shape
    group_ends = jnp.cumsum(star_counts)
    group_starts = group_ends - star_counts
    flat_cells = star_cells.reshape(-1)
    flat_bands = star_bands.reshape(-1)
    cell_count = coef_table.shape[0]
    capacity = -(-slot_count // groups)
    targets = jnp.arange(groups, dtype=jnp.int32)
    lane_index = jnp.arange(capacity, dtype=jnp.int32)
    my_start = table_pick(group_starts, my_group[None])
    my_count = table_pick(star_counts, my_group[None])
    first_slot = (targets - my_start) % groups
    send_slot = (first_slot[:, None] + lane_index[None, :] * groups).reshape(-1)
    valid_mask = send_slot < my_count
    picked = jnp.take(psf_cotangent, jnp.minimum(send_slot, slot_count - 1), axis=0)
    outgoing = jnp.where(valid_mask[:, None, None], picked, jnp.zeros_like(picked))
    incoming = lax.all_to_all(outgoing, "star", split_axis=0, concat_axis=0, tiled=True)
    star_rank = my_group + jnp.arange(LIVE_DEV, dtype=jnp.int32) * groups
    owner_group = jnp.sum((group_ends[None, :] <= star_rank[:, None]).astype(jnp.int32), axis=1)
    within = star_rank - table_pick(group_starts, owner_group)
    live_mask = jnp.ones((LIVE_DEV,), dtype=bool)
    owner_group, within, live_mask = (owner_group, within, live_mask)
    cotangent = jnp.take(incoming, owner_group * capacity + within // groups, axis=0)
    slot_index = owner_group * slot_count + within
    cell_ids = table_pick(flat_cells, slot_index)
    band_ids = table_pick(flat_bands, slot_index)
    cell_hot = cell_ids[:, None] == jnp.arange(cell_count, dtype=jnp.int32)[None, :]
    coef_rows = jnp.dot(
        cell_hot.astype(jnp.bfloat16), coef_table, preferred_element_type=jnp.float32
    ).astype(jnp.bfloat16)
    flat_maps = feature_maps.reshape(map_count, row_count * pupil_size)
    path_error = jnp.dot(coef_rows, flat_maps, preferred_element_type=jnp.float32).reshape(
        -1, row_count, pupil_size
    )
    wave_number = wave_numbers(band_ids)
    phase_angle = wave_number[:, None, None] * path_error
    aperture = aperture_rows(lax.axis_index("row") * row_count, row_count, pupil_size)
    cos_phase = jnp.cos(phase_angle)
    sin_phase = jnp.sin(phase_angle)
    pupil_field = jnp.stack([aperture * cos_phase, aperture * sin_phase], 1).astype(jnp.bfloat16)
    cos_table, sin_table = fourier_tables(pupil_size)
    inverse = 1.0 / pupil_size
    along_cos = jnp.einsum(
        "sarc,cv->sarv", pupil_field, cos_table, preferred_element_type=jnp.float32
    )
    along_sin = jnp.einsum(
        "sarc,cv->sarv", pupil_field, sin_table, preferred_element_type=jnp.float32
    )
    column_field = jnp.stack(
        [along_cos[:, 0] - along_sin[:, 1], along_sin[:, 0] + along_cos[:, 1]], 1
    ).astype(jnp.bfloat16)
    pieces = lax.all_to_all(column_field, "row", split_axis=3, concat_axis=2, tiled=True)
    row_cos = jnp.einsum("sarv,ru->savu", pieces, cos_table, preferred_element_type=jnp.float32)
    row_sin = jnp.einsum("sarv,ru->savu", pieces, sin_table, preferred_element_type=jnp.float32)
    real_part = (row_cos[:, 0] - row_sin[:, 1]) * inverse
    imag_part = (row_sin[:, 0] + row_cos[:, 1]) * inverse
    focal_field = jnp.stack([real_part, imag_part], 1)
    weight = jnp.where(live_mask, 2.0, 0.0).astype(jnp.float32)[:, None, None, None]
    focal_grad = (weight * cotangent.astype(jnp.float32)[:, None] * focal_field).astype(
        jnp.bfloat16
    )
    back_cos = jnp.einsum(
        "savu,ur->savr", focal_grad, cos_table, preferred_element_type=jnp.float32
    )
    back_sin = jnp.einsum(
        "savu,ur->savr", focal_grad, sin_table, preferred_element_type=jnp.float32
    )
    spectrum_grad = jnp.stack(
        [(back_cos[:, 0] + back_sin[:, 1]) * inverse, (back_cos[:, 1] - back_sin[:, 0]) * inverse],
        1,
    ).astype(jnp.bfloat16)
    pieces = lax.all_to_all(spectrum_grad, "row", split_axis=3, concat_axis=2, tiled=True)
    col_cos = jnp.einsum("savr,vc->sarc", pieces, cos_table, preferred_element_type=jnp.float32)
    col_sin = jnp.einsum("savr,vc->sarc", pieces, sin_table, preferred_element_type=jnp.float32)
    pupil_grad = jnp.stack([col_cos[:, 0] + col_sin[:, 1], col_cos[:, 1] - col_sin[:, 0]], 1)
    phase_grad = aperture * (cos_phase * pupil_grad[:, 1] - sin_phase * pupil_grad[:, 0])
    path_grad = (
        (wave_number[:, None, None] * phase_grad)
        .astype(jnp.bfloat16)
        .reshape(-1, row_count * pupil_size)
    )
    map_scores = lax.dot_general(
        path_grad, flat_maps, (((1,), (1,)), ((), ())), preferred_element_type=jnp.float32
    )
    coef_part = lax.dot_general(
        cell_hot.astype(jnp.float32),
        map_scores * (1.0 / (8 * pupil_size)),
        (((0,), (0,)), ((), ())),
        precision=lax.Precision.HIGHEST,
    )
    coef_grad = lax.psum(coef_part, ("star", "row"))
    share = map_count // groups
    map_grad = lax.psum_scatter(
        lax.dot_general(
            coef_rows, path_grad, (((0,), (0,)), ((), ())), preferred_element_type=jnp.float32
        ),
        "star",
        scatter_dimension=0,
        tiled=True,
    )
    return (map_grad.reshape(share, row_count, pupil_size), coef_grad)


def quarter_tables(size):
    quarter = size // RADIX
    place = np.arange(quarter)[None, :, None]
    freq = RADIX * np.arange(quarter)[None, None, :] + np.arange(RADIX)[:, None, None]
    angle = 2.0 * np.pi / size * ((place * freq) % size)
    cosine, sine = np.cos(angle), -np.sin(angle)
    right = np.concatenate(
        [np.concatenate([cosine, sine], 2), np.concatenate([-sine, cosine], 2)], 1
    ).astype(np.float32)
    left = np.swapaxes(right, 1, 2)
    return jnp.asarray(right.astype(jnp.bfloat16)), jnp.asarray(left.astype(jnp.bfloat16))


def turn_cos_sin(turns):
    half = turns * np.float32(np.pi)
    square = half * half
    sine = jnp.full_like(square, -1.0 / 39916800.0)
    for term in (1.0 / 362880.0, -1.0 / 5040.0, 1.0 / 120.0, -1.0 / 6.0, 1.0):
        sine = sine * square + np.float32(term)
    sine = sine * half
    cosine = jnp.full_like(square, 1.0 / 479001600.0)
    for term in (-1.0 / 3628800.0, 1.0 / 40320.0, -1.0 / 720.0, 1.0 / 24.0, -0.5, 1.0):
        cosine = cosine * square + np.float32(term)
    return 1.0 - 2.0 * sine * sine, 2.0 * sine * cosine


def butterfly(real, imag, sign):
    sr, dr = real[0] + real[2], real[0] - real[2]
    si, di = imag[0] + imag[2], imag[0] - imag[2]
    tr, er = real[1] + real[3], real[1] - real[3]
    ti, ei = imag[1] + imag[3], imag[1] - imag[3]
    if sign < 0:
        er, ei = -er, -ei
    return (
        [sr + tr, dr - ei, sr - tr, dr + ei],
        [si + ti, di + er, si - ti, di - er],
    )


def phase_kernel(inverse_ref, weight_ref, maps_ref, out_ref):
    stars, rows, size = out_ref.shape
    maps = maps_ref[...].reshape(maps_ref.shape[0] * rows, size)
    path = jnp.dot(weight_ref[...], maps, preferred_element_type=F32)
    for star in range(stars):
        turns = path[star * rows : (star + 1) * rows] * inverse_ref[star]
        out_ref[star] = (turns - jnp.floor(turns + 0.5)).astype(BF16)


def phase_turns(inverse_wave, coef_rows, feature_maps):
    map_count, row_count, size = feature_maps.shape
    stars = coef_rows.shape[0]
    weights = spread_rows(coef_rows)
    return pl.pallas_call(
        phase_kernel,
        out_shape=jax.ShapeDtypeStruct((stars, row_count, size), BF16),
        grid=(row_count // ROWS_STEP,),
        in_specs=[
            pl.BlockSpec(memory_space=pltpu.SMEM),
            pl.BlockSpec(weights.shape, lambda i: (0, 0)),
            pl.BlockSpec((map_count, ROWS_STEP, size), lambda i: (0, i, 0)),
        ],
        out_specs=pl.BlockSpec((stars, ROWS_STEP, size), lambda i: (0, i, 0)),
        cost_estimate=pl.CostEstimate(
            flops=2 * stars * ROWS_STEP * map_count * row_count * size,
            bytes_accessed=2 * (map_count + stars) * row_count * size,
            transcendentals=0,
        ),
        compiler_params=pltpu.CompilerParams(vmem_limit_bytes=24 << 20),
        name="phase_turns",
    )(inverse_wave, weights, feature_maps)


def spread_rows(weights):
    eye = jnp.eye(ROWS_STEP, dtype=weights.dtype)
    outs, ins = weights.shape
    spread = weights[:, None, :, None] * eye[None, :, None, :]
    return spread.reshape(outs * ROWS_STEP, ins * ROWS_STEP)


def star_kernel(
    chunk, wave_ref, turns_ref, cot_ref, right_ref, left_ref, out_ref, pr, pi, yr, yi, ct, xr, xi
):
    size = turns_ref.shape[1]
    quarter = size // RADIX
    steps = size // chunk
    blocks = [slice(m * quarter, (m + 1) * quarter) for m in range(RADIX)]
    centre = 0.5 * (size - 1)
    scale = 1.0 / size

    def forward_columns(step, carry):
        rows = pl.ds(pl.multiple_of(step * chunk, chunk), chunk)
        cosine, sine = turn_cos_sin(turns_ref[rows, :].astype(F32))
        row_pos = (
            lax.broadcasted_iota(jnp.int32, (chunk, size), 0) + step * chunk
        ).astype(F32) - centre
        col_pos = lax.broadcasted_iota(jnp.int32, (chunk, size), 1).astype(F32) - centre
        inside = row_pos * row_pos + col_pos * col_pos <= 0.25 * size * size
        real = jnp.where(inside, cosine, 0.0)
        imag = jnp.where(inside, sine, 0.0)
        pr[rows, :] = real
        pi[rows, :] = imag
        mixed_real, mixed_imag = butterfly(
            [real[:, b] for b in blocks], [imag[:, b] for b in blocks], -1
        )
        for k in range(RADIX):
            both = jnp.concatenate([mixed_real[k].astype(BF16), mixed_imag[k].astype(BF16)], 1)
            made = jnp.dot(both, right_ref[k], preferred_element_type=F32).astype(BF16)
            yr[rows, blocks[k]] = made[:, :quarter]
            yi[rows, blocks[k]] = made[:, quarter:]
        return carry

    lax.fori_loop(0, steps, forward_columns, 0)

    def pick(k):
        j = lax.broadcasted_iota(jnp.int32, (quarter, size), 0)
        f = lax.broadcasted_iota(jnp.int32, (quarter, size), 1)
        return jnp.where(f == RADIX * j + k, 1.0, 0.0).astype(BF16)

    nt = (((1,), (1,)), ((), ()))
    for k in range(RADIX):
        part = lax.dot_general(
            pick(k), cot_ref[...], nt, preferred_element_type=F32
        ).astype(BF16)
        for m in range(RADIX):
            ct[blocks[k], blocks[m]] = lax.dot_general(
                part, pick(m), nt, preferred_element_type=F32
            )

    def focal(step, carry):
        cols = pl.ds(pl.multiple_of(step * quarter, quarter), quarter)
        mixed_real, mixed_imag = butterfly(
            [yr[b, cols].astype(F32) for b in blocks],
            [yi[b, cols].astype(F32) for b in blocks],
            -1,
        )
        back_real, back_imag = [], []
        for k in range(RADIX):
            both = jnp.concatenate([mixed_real[k].astype(BF16), mixed_imag[k].astype(BF16)], 0)
            field = jnp.dot(left_ref[k], both, preferred_element_type=F32)
            weight = ct[blocks[k], cols] * (2.0 * scale)
            grad = (field * jnp.concatenate([weight, weight], 0)).astype(BF16)
            back = jnp.dot(right_ref[k], grad, preferred_element_type=F32)
            back_real.append(back[:quarter])
            back_imag.append(back[quarter:])
        spec_real, spec_imag = butterfly(back_real, back_imag, 1)
        for m in range(RADIX):
            xr[blocks[m], cols] = (spec_real[m] * scale).astype(BF16)
            xi[blocks[m], cols] = (spec_imag[m] * scale).astype(BF16)
        return carry

    lax.fori_loop(0, RADIX, focal, 0)

    def inverse_columns(step, carry):
        rows = pl.ds(pl.multiple_of(step * chunk, chunk), chunk)
        part_real, part_imag = [], []
        for k in range(RADIX):
            both = jnp.concatenate([xr[rows, blocks[k]], xi[rows, blocks[k]]], 1)
            made = jnp.dot(both, left_ref[k], preferred_element_type=F32)
            part_real.append(made[:, :quarter])
            part_imag.append(made[:, quarter:])
        grad_real, grad_imag = butterfly(part_real, part_imag, 1)
        wave = wave_ref[0]
        for m in range(RADIX):
            grad = pr[rows, blocks[m]] * grad_imag[m] - pi[rows, blocks[m]] * grad_real[m]
            out_ref[rows, blocks[m]] = (wave * grad).astype(BF16)
        return carry

    lax.fori_loop(0, steps, inverse_columns, 0)


def star_gradient(wave, turns, cotangent, right, left):
    size = turns.shape[0]
    vmem = pl.BlockSpec(memory_space=pltpu.VMEM)
    square = (size, size)
    return pl.pallas_call(
        functools.partial(star_kernel, 128),
        out_shape=jax.ShapeDtypeStruct(square, BF16),
        in_specs=[pl.BlockSpec(memory_space=pltpu.SMEM), vmem, vmem, vmem, vmem],
        out_specs=vmem,
        scratch_shapes=[
            pltpu.VMEM(square, F32),
            pltpu.VMEM(square, F32),
            pltpu.VMEM(square, BF16),
            pltpu.VMEM(square, BF16),
            pltpu.VMEM(square, F32),
            pltpu.VMEM(square, BF16),
            pltpu.VMEM(square, BF16),
        ],
        compiler_params=pltpu.CompilerParams(vmem_limit_bytes=56 << 20),
        name="star_gradient",
    )(wave, turns, cotangent, right, left)


def maps_kernel(group_ref, weight_ref, grad_ref, maps_ref, out_ref, score_ref):
    share, rows, size = out_ref.shape
    grads = grad_ref[...].reshape(grad_ref.shape[0] * rows, size)
    maps = maps_ref[...].reshape(share * rows, size)
    total = jnp.dot(weight_ref[...], grads, preferred_element_type=F32)
    out_ref[...] = total.reshape(share, rows, size)

    @pl.when(pl.program_id(0) == 0)
    def _():
        score_ref[...] = jnp.zeros_like(score_ref)

    score_ref[...] += lax.dot_general(
        maps, grads, (((1,), (1,)), ((), ())), preferred_element_type=F32
    )


def map_sums(my_group, coef_rows, path_grads, feature_maps, share):
    stars, row_count, size = path_grads.shape
    weights = spread_rows(coef_rows)
    score_shape = (share * ROWS_STEP, stars * ROWS_STEP)
    map_grad, scores = pl.pallas_call(
        maps_kernel,
        out_shape=(
            jax.ShapeDtypeStruct((share, row_count, size), F32),
            jax.ShapeDtypeStruct(score_shape, F32),
        ),
        grid_spec=pltpu.PrefetchScalarGridSpec(
            num_scalar_prefetch=1,
            grid=(row_count // ROWS_STEP,),
            in_specs=[
                pl.BlockSpec(weights.shape, lambda i, g: (0, 0)),
                pl.BlockSpec((stars, ROWS_STEP, size), lambda i, g: (0, i, 0)),
                pl.BlockSpec((share, ROWS_STEP, size), lambda i, g: (g[0], i, 0)),
            ],
            out_specs=(
                pl.BlockSpec((share, ROWS_STEP, size), lambda i, g: (0, i, 0)),
                pl.BlockSpec(score_shape, lambda i, g: (0, 0)),
            ),
        ),
        compiler_params=pltpu.CompilerParams(vmem_limit_bytes=56 << 20),
        name="map_sums",
    )(my_group[None], weights, path_grads, feature_maps)
    eye = jnp.eye(ROWS_STEP, dtype=F32)
    scores = scores.reshape(share, ROWS_STEP, stars, ROWS_STEP)
    return map_grad, jnp.sum(scores * eye[None, :, None, :], axis=(1, 3))


GATHER_STEPS = 8


def greet(peers):
    barrier = pltpu.get_barrier_semaphore()
    for peer in peers:
        pl.semaphore_signal(barrier, inc=1, device_id=peer, device_id_type=pl.DeviceIdType.MESH)
    pl.semaphore_wait(barrier, len(peers))


def send(source, target, send_sem, recv_sem, peer):
    return pltpu.make_async_remote_copy(
        src_ref=source,
        dst_ref=target,
        send_sem=send_sem,
        recv_sem=recv_sem,
        device_id=peer,
        device_id_type=pl.DeviceIdType.MESH,
    )


DELIVER_STEPS = 4


def deliver_kernel(
    groups, lanes, pick_ref, turns_ref, cot_ref, turns_out, cot_out, stage, *scratch
):
    arrived, sems = scratch[:DELIVER_STEPS], scratch[DELIVER_STEPS:]
    t_local, t_send, t_recv, s_local, s_send, s_recv, z_local, z_send, z_recv = sems
    row = lax.axis_index("row")
    me = lax.axis_index("star")
    capacity = cot_ref.shape[1]
    depth = cot_ref.shape[2] // DELIVER_STEPS
    row_peers = [{"row": (row + d) % lanes} for d in range(1, lanes)]
    star_peers = [{"star": (me + d) % groups} for d in range(1, groups)]
    greet(row_peers + star_peers)
    turns = [
        send(
            turns_ref.at[(row + d) % lanes],
            turns_out.at[row],
            t_send.at[d - 1],
            t_recv.at[d - 1],
            row_peers[d - 1],
        )
        for d in range(1, lanes)
    ]
    turns.append(pltpu.make_async_copy(turns_ref.at[row], turns_out.at[row], t_local))
    for copy in turns:
        copy.start()
    steps = []
    for step in range(DELIVER_STEPS):
        rows = pl.ds(step * depth, depth)
        target = arrived[step].at[pl.ds(me * capacity, capacity)]
        copies = [
            send(
                cot_ref.at[(me + d) % groups, :, rows],
                target,
                s_send.at[step, d - 1],
                s_recv.at[step, d - 1],
                star_peers[d - 1],
            )
            for d in range(1, groups)
        ]
        copies.append(pltpu.make_async_copy(cot_ref.at[me, :, rows], target, s_local.at[step]))
        for copy in copies:
            copy.start()
        steps.append(copies)
    sent = []
    for step in range(DELIVER_STEPS):
        rows = pl.ds(step * depth, depth)
        for copy in steps[step]:
            copy.wait()
        for lane in range(lanes):
            stage[lane, rows] = arrived[step][pick_ref[lane]]
        copies = [
            send(
                stage.at[(row + d) % lanes, rows],
                cot_out.at[row, rows],
                z_send.at[step, d - 1],
                z_recv.at[step, d - 1],
                row_peers[d - 1],
            )
            for d in range(1, lanes)
        ]
        copies.append(
            pltpu.make_async_copy(stage.at[row, rows], cot_out.at[row, rows], z_local.at[step])
        )
        for copy in copies:
            copy.start()
        sent += copies
    for copy in turns + sent:
        copy.wait()


def deliver(picks, turns, outgoing):
    groups, capacity, row_count, size = outgoing.shape
    lanes = turns.shape[0]
    depth = row_count // DELIVER_STEPS
    dma = pltpu.SemaphoreType.DMA
    hbm = pl.BlockSpec(memory_space=pl.ANY)
    vmem = pl.BlockSpec(memory_space=pltpu.VMEM)
    shape = jax.ShapeDtypeStruct((lanes, row_count, size), BF16)
    return pl.pallas_call(
        functools.partial(deliver_kernel, groups, lanes),
        out_shape=(shape, shape),
        in_specs=[pl.BlockSpec(memory_space=pltpu.SMEM), vmem, hbm],
        out_specs=(hbm, hbm),
        scratch_shapes=[pltpu.VMEM((lanes, row_count, size), BF16)]
        + [pltpu.VMEM((groups * capacity, depth, size), BF16)] * DELIVER_STEPS
        + [
            dma,
            dma((lanes - 1,)),
            dma((lanes - 1,)),
            dma((DELIVER_STEPS,)),
            dma((DELIVER_STEPS, groups - 1)),
            dma((DELIVER_STEPS, groups - 1)),
            dma((DELIVER_STEPS,)),
            dma((DELIVER_STEPS, lanes - 1)),
            dma((DELIVER_STEPS, lanes - 1)),
        ],
        compiler_params=pltpu.CompilerParams(
            collective_id=0, has_side_effects=True, vmem_limit_bytes=56 << 20
        ),
        name="deliver",
    )(picks, turns, outgoing)


def gather_kernel(lanes, in_ref, out_ref, local, z_send, z_recv, p_send, p_recv, c_send, c_recv):
    row = lax.axis_index("row")
    me = lax.axis_index("star")
    depth = in_ref.shape[1] // GATHER_STEPS
    core = me + 1 - 2 * (me % 2)
    across = me + 2 - 4 * ((me // 2) % 2)
    along = me + 4 - 8 * ((me // 4) % 2)
    corner = across + 4 - 8 * ((me // 4) % 2)
    peers = [{"row": (row + d) % lanes} for d in range(1, lanes)]
    to_core, to_across, to_along = {"star": core}, {"star": across}, {"star": along}
    greet(peers + [to_core, to_across, to_along])
    half = lanes // 2
    started = []

    def start(copy):
        copy.start()
        started.append(copy)
        return copy

    def block(group, step, first=0, count=lanes):
        return out_ref.at[group, pl.ds(first, count), pl.ds(step * depth, depth)]

    own, exchanged = [], []
    for step in range(GATHER_STEPS):
        rows = pl.ds(step * depth, depth)
        copy = pltpu.make_async_copy(
            in_ref.at[row, rows], out_ref.at[me, row, rows], local.at[step]
        )
        copy.start()
        own.append(copy)
        exchanged.append(
            [
                start(
                    send(
                        in_ref.at[(row + d) % lanes, rows],
                        out_ref.at[me, row, rows],
                        z_send.at[step, d - 1],
                        z_recv.at[step, d - 1],
                        peers[d - 1],
                    )
                )
                for d in range(1, lanes)
            ]
        )

    def plane(step, way, part, peer):
        return start(send(part, part, p_send.at[step, way], p_recv.at[step, way], peer))

    def cores(step, way, part):
        return start(send(part, part, c_send.at[step, way], c_recv.at[step, way], to_core))

    sides, corners, twins = {}, {}, []
    for step in range(GATHER_STEPS + 2):
        if step < GATHER_STEPS:
            own[step].wait()
            for copy in exchanged[step]:
                copy.wait_recv()
            part = block(me, step)
            sides[step] = (
                plane(step, 0, part, to_across),
                plane(step, 1, part, to_along),
            )
            twins.append(cores(step, 0, part))
        last = step - 1
        if 0 <= last < GATHER_STEPS:
            sides[last][0].wait_recv()
            first = plane(last, 2, block(across, last, 0, half), to_along)
            twins.append(cores(last, 1, block(across, last)))
            sides[last][1].wait_recv()
            second = plane(last, 3, block(along, last, half, lanes - half), to_across)
            twins.append(cores(last, 2, block(along, last)))
            corners[last] = (first, second)
        last = step - 2
        if last >= 0:
            corners[last][0].wait_recv()
            corners[last][1].wait_recv()
            twins.append(cores(last, 3, block(corner, last)))
    for copy in twins:
        copy.wait_recv()
    for copy in started:
        copy.wait_send()


def gather_grads(path_grad, groups):
    lanes, row_count, size = path_grad.shape
    dma = pltpu.SemaphoreType.DMA
    return pl.pallas_call(
        functools.partial(gather_kernel, lanes),
        out_shape=jax.ShapeDtypeStruct((groups, lanes, row_count, size), path_grad.dtype),
        in_specs=[pl.BlockSpec(memory_space=pltpu.VMEM)],
        out_specs=pl.BlockSpec(memory_space=pl.ANY),
        scratch_shapes=[
            dma((GATHER_STEPS,)),
            dma((GATHER_STEPS, lanes - 1)),
            dma((GATHER_STEPS, lanes - 1)),
            dma((GATHER_STEPS, 4)),
            dma((GATHER_STEPS, 4)),
            dma((GATHER_STEPS, 4)),
            dma((GATHER_STEPS, 4)),
        ],
        compiler_params=pltpu.CompilerParams(
            collective_id=1, has_side_effects=True, vmem_limit_bytes=56 << 20
        ),
        name="gather_grads",
    )(path_grad)


def score_kernel(groups, lanes, in_ref, out_ref, z_send, z_recv, s_send, s_recv):
    row = lax.axis_index("row")
    me = lax.axis_index("star")
    row_peers = [{"row": (row + d) % lanes} for d in range(1, lanes)]
    star_peers = [{"star": (me + d) % groups} for d in range(1, groups)]
    greet(row_peers + star_peers)
    copies = [
        send(in_ref, out_ref.at[me, row], z_send.at[d], z_recv.at[d], row_peers[d])
        for d in range(lanes - 1)
    ]
    for copy in copies:
        copy.start()
    out_ref[me, row] = in_ref[...]
    for copy in copies:
        copy.wait()
    copies = [
        send(out_ref.at[me], out_ref.at[me], s_send.at[d], s_recv.at[d], star_peers[d])
        for d in range(groups - 1)
    ]
    for copy in copies:
        copy.start()
    for copy in copies:
        copy.wait()


def gather_scores(scores, groups, lanes):
    dma = pltpu.SemaphoreType.DMA
    vmem = pl.BlockSpec(memory_space=pltpu.VMEM)
    return pl.pallas_call(
        functools.partial(score_kernel, groups, lanes),
        out_shape=jax.ShapeDtypeStruct((groups, lanes) + scores.shape, scores.dtype),
        in_specs=[vmem],
        out_specs=vmem,
        scratch_shapes=[
            dma((lanes - 1,)),
            dma((lanes - 1,)),
            dma((groups - 1,)),
            dma((groups - 1,)),
        ],
        compiler_params=pltpu.CompilerParams(
            collective_id=2, has_side_effects=True, vmem_limit_bytes=8 << 20
        ),
        name="gather_scores",
    )(scores)


def star_devices(feature_maps, coef_table, star_counts, star_cells, star_bands, psf_cotangent):
    groups = lax.axis_size("star")
    lanes = lax.axis_size("row")
    my_group = lax.axis_index("star")
    my_lane = lax.axis_index("row")
    slot_count = psf_cotangent.shape[0]
    map_count, row_count, size = feature_maps.shape
    cell_count = coef_table.shape[0]
    share = map_count // groups
    group_ends = jnp.cumsum(star_counts)
    group_starts = group_ends - star_counts
    capacity = -(-slot_count // groups)
    targets = jnp.arange(groups, dtype=jnp.int32)
    my_start = table_pick(group_starts, my_group[None])
    first_slot = (targets - my_start) % groups
    lane_index = jnp.arange(capacity, dtype=jnp.int32)
    send_slot = (first_slot[:, None] + lane_index[None, :] * groups).reshape(-1)
    outgoing = jnp.take(
        psf_cotangent, jnp.minimum(send_slot, slot_count - 1), axis=0, mode="clip"
    )
    outgoing = outgoing.reshape((groups, capacity) + outgoing.shape[1:])

    total = groups * lanes
    order = jnp.arange(total, dtype=jnp.int32)
    rank = order // lanes + (order % lanes) * groups
    owner = jnp.sum((group_ends[None, :] <= rank[:, None]).astype(jnp.int32), axis=1)
    within = rank - table_pick(group_starts, owner)
    slot_index = owner * slot_count + within
    cell_ids = table_pick(star_cells.reshape(-1), slot_index)
    band_ids = table_pick(star_bands.reshape(-1), slot_index)
    cell_hot = cell_ids[:, None] == jnp.arange(cell_count, dtype=jnp.int32)[None, :]
    coef_rows = jnp.dot(
        cell_hot.astype(BF16), coef_table, preferred_element_type=F32
    ).astype(BF16)

    def mine(values):
        return lax.dynamic_slice_in_dim(values, my_group * lanes, lanes, 0)

    wavelength = 0.55 + 0.35 * band_ids.astype(F32) / (BANDS - 1)
    turns = phase_turns(mine(1.0 / wavelength), mine(coef_rows), feature_maps)
    picks = mine(owner) * capacity + mine(within) // groups
    turns, cotangent = deliver(picks, turns, outgoing)
    wave = wave_numbers(band_ids)
    my_wave = lax.dynamic_slice_in_dim(wave, my_group * lanes + my_lane, 1, 0)
    right, left = quarter_tables(size)
    path_grad = star_gradient(
        my_wave, turns.reshape(size, size), cotangent.reshape(size, size), right, left
    )
    path_grads = gather_grads(path_grad.reshape(lanes, row_count, size), groups)
    path_grads = path_grads.reshape(total, row_count, size)
    my_coefs = lax.dynamic_slice_in_dim(coef_rows.T, my_group * share, share, 0)
    map_grad, scores = map_sums(my_group, my_coefs, path_grads, feature_maps, share)
    scores = jnp.pad(scores, ((0, 0), (0, -total % 128)))
    scores = jnp.sum(gather_scores(scores, groups, lanes), axis=1)
    scores = scores.reshape(map_count, -1)[:, :total]
    coef_grad = lax.dot_general(
        cell_hot.astype(F32),
        scores * (1.0 / (8 * size)),
        (((0,), (1,)), ((), ())),
        precision=lax.Precision.HIGHEST,
    )
    return map_grad, coef_grad


def solution(mesh):
    placed = (P(None, "row", None), P(), P(), P(), P(), P("star", "row", None))
    fits = mesh.shape["row"] == LIVE_DEV and mesh.shape["star"] == PLANE_DEV
    device = star_devices if fits else per_device
    return jax.shard_map(
        device,
        mesh=mesh,
        in_specs=placed,
        out_specs=(P("star", "row", None), P()),
        check_vma=False,
    )
```

profile of v0, /device:TPU:27, one launch (start us, length us, event | category | flops | bytes accessed | tf_op | source)
XLA Modules:
  0.0 299.1 jit_solution(1404273143138238085)
XLA Ops:
  0.7 0.8 reduce-window.8
  1.5 1.3 fusion.10
  3.0 0.8 broadcast_in_dim.66
  3.7 0.8 broadcast_in_dim.69
  4.5 0.2 select_reduce_fusion
  4.7 0.2 convolution_convert_fusion
  4.9 0.1 broadcast_multiply_fusion
  5.1 1.8 mul.110.weight_ref
  6.9 18.7 %phase_turns.1.turns_ref = bf16[4,256,1024]{2,1,0:T(8,128)(2,1)S(1)} custom-call(f32[4]{0:T(128)S(1)} %dynamic_slice.22.inverse_ref, bf16[64,1024]{1,0:T(8,128)(2,1)S(1)} %mul.110.weight_ref, bf16[64,256,1024]{2,1,0:T(8,128)(2,1)} %maps_ref.3), custom_call_target="tpu_custom_call" | custom-call | flops 2147483648 | bytes 35651584 | tf_op jit(solution)/shard_map/phase_turns/pallas_call | solution.py:205
  25.6 1.3 copy-done.2
  27.0 0.6 fusion.12.pick_ref
  27.6 0.7 and_select_fusion
  28.4 7.7 %gather_fusion = bf16[16,256,1024]{2,1,0:T(8,128)(2,1)} fusion(bf16[12,256,1024]{2,1,0:T(8,128)(2,1)} %param.13, s32[1024]{0:T(1024)S(1)} %pad_clamp_fusion), kind=kCustom, calls=%fused_computation | custom fusion | bytes 16777280 | tf_op jit(solution)/shard_map/jit(_take)/gather | solution.py:690
  36.1 108.7 %deliver.1 = (bf16[4,256,1024]{2,1,0:T(8,128)(2,1)}, bf16[4,256,1024]{2,1,0:T(8,128)(2,1)}) custom-call(s32[4]{0:T(128)} %fusion.12.pick_ref, bf16[4,256,1024]{2,1,0:T(8,128)(2,1)} %copy-done.2, bf16[8,2,256,1024]{3,2,1,0:T(8,128)(2,1)} %bitcast.19), custom_call_target="tpu_custom_call" | custom-call | tf_op jit(solution)/shard_map/deliver/pallas_call | solution.py:495
  144.8 0.6 dynamic_slice.19.wave_ref
  145.3 29.9 %star_gradient.1 = bf16[1024,1024]{1,0:T(8,128)(2,1)} custom-call(f32[1]{0:T(128)} %dynamic_slice.19.wave_ref, bf16[1024,1024]{1,0:T(8,128)(2,1)} %bitcast.21, bf16[1024,1024]{1,0:T(8,128)(2,1)} %bitcast.22, bf16[4,512,512]{2,1,0:T(8,128)(2,1)} %constant.106.clone.right_ref, bf16[4,512,512]{2,1,0:T(8,128)(2,1)} %constant.107.clone.left_ref), custom_call_target="tpu_custom_call" | custom-call | tf_op jit(solution)/shard_map/star_gradient/pallas_call | solution.py:327
  175.3 85.3 %gather_grads.1 = bf16[8,4,256,1024]{3,2,1,0:T(8,128)(2,1)} custom-call(bf16[4,256,1024]{2,1,0:T(8,128)(2,1)} %bitcast.20), custom_call_target="tpu_custom_call" | custom-call | tf_op jit(solution)/shard_map/gather_grads/pallas_call | solution.py:606
  260.8 0.1 broadcast_multiply_fusion.1
  260.9 2.5 mul.104.weight_ref
  263.4 20.4 %map_sums.1 = (f32[8,256,1024]{2,1,0:T(8,128)}, f32[128,512]{1,0:T(8,128)}) custom-call(s32[1]{0:T(128)} %bitcast.group_ref, bf16[128,512]{1,0:T(8,128)(2,1)} %mul.104.weight_ref, bf16[32,256,1024]{2,1,0:T(8,128)(2,1)} %bitcast.18, bf16[64,256,1024]{2,1,0:T(8,128)(2,1)} %maps_ref.3), custom_call_target="tpu_custom_call" | custom-call | tf_op jit(solution)/shard_map/map_sums/pallas_call | solution.py:366
  283.8 1.8 reshape.168
  285.6 0.3 multiply_reduce_fusion
  285.9 12.3 %gather_scores.1 = f32[8,4,8,128]{3,2,1,0:T(8,128)S(1)} custom-call(f32[8,128]{1,0:T(8,128)S(1)} %pad.4.in_ref), custom_call_target="tpu_custom_call" | custom-call | tf_op jit(solution)/shard_map/gather_scores/pallas_call | solution.py:655
  298.2 0.9 fusion
  (22 shorter events, 0.7 us)
Async XLA Ops:
  0.6 4.1 %copy-start = (bf16[64,64]{1,0:T(8,128)(2,1)S(1)}, bf16[64,64]{1,0:T(8,128)(2,1)}, u32[]{:S(2)}) copy-start(bf16[64,64]{1,0:T(8,128)(2,1)} %param.9) | copy-start | bytes 24580
  25.6 1.3 copy-start.2
  283.8 15.4 %copy-start.1 = (bf16[64,64]{1,0:T(8,128)(2,1)S(1)}, bf16[64,64]{1,0:T(8,128)(2,1)}, u32[]{:S(2)}) copy-start(bf16[64,64]{1,0:T(8,128)(2,1)} %param.9) | copy-start | bytes 24580
where the time goes:
time: 303 us; the launch traced here: 299 us
  Pallas kernels  275 us (91%)
  local copies, waits for them, and re-layouts  17.5 us (6%)
  other arithmetic  4.47 us (1%)
    pallas_call x1, Pallas kernels, deliver(): pl.pallas_call(functools.partial(deliver_kernel, groups, lanes), out_shap...  109 us
    pallas_call x1, Pallas kernels, gather_grads(): pl.pallas_call(functools.partial(gather_kernel, lanes), out_shape=jax.Sha...  85.3 us
    pallas_call x1, Pallas kernels, star_gradient(): pl.pallas_call(functools.partial(star_kernel, 128), out_shape=jax.ShapeDt...  29.9 us
    pallas_call x1, Pallas kernels, map_sums(): pl.pallas_call(maps_kernel, out_shape=(jax.ShapeDtypeStruct((share, row_c...  20.4 us
    pallas_call x1, Pallas kernels, phase_turns(): pl.pallas_call(phase_kernel, out_shape=jax.ShapeDtypeStruct((stars, row_c...  18.7 us
    pallas_call x1, Pallas kernels, gather_scores(): pl.pallas_call(functools.partial(score_kernel, groups, lanes), out_shape=...  12.3 us
    gather x1, local copies, waits for them, and re-layouts, star_devices(): jnp.take(psf_cotangent, jnp.minimum(send_slot, slot_count - 1), axis=0, m...  7.69 us

commit v1 on v0

--- a/solution.py
+++ b/solution.py
@@ -13,6 +13,12 @@
 PLANE_DEV = 8
 RADIX = 4
 ROWS_STEP = 16
+TURN_STEPS = 8
+EARLY_STEPS = 2
+ROUTE_CHUNKS = 8
+OVER_X = 11
+OVER_Y = 6
+STARS_CHIP = 8
 F32 = jnp.float32
 BF16 = jnp.bfloat16
 
@@ -189,158 +195,11 @@
     )
 
 
-def phase_kernel(inverse_ref, weight_ref, maps_ref, out_ref):
-    stars, rows, size = out_ref.shape
-    maps = maps_ref[...].reshape(maps_ref.shape[0] * rows, size)
-    path = jnp.dot(weight_ref[...], maps, preferred_element_type=F32)
-    for star in range(stars):
-        turns = path[star * rows : (star + 1) * rows] * inverse_ref[star]
-        out_ref[star] = (turns - jnp.floor(turns + 0.5)).astype(BF16)
-
-
-def phase_turns(inverse_wave, coef_rows, feature_maps):
-    map_count, row_count, size = feature_maps.shape
-    stars = coef_rows.shape[0]
-    weights = spread_rows(coef_rows)
-    return pl.pallas_call(
-        phase_kernel,
-        out_shape=jax.ShapeDtypeStruct((stars, row_count, size), BF16),
-        grid=(row_count // ROWS_STEP,),
-        in_specs=[
-            pl.BlockSpec(memory_space=pltpu.SMEM),
-            pl.BlockSpec(weights.shape, lambda i: (0, 0)),
-            pl.BlockSpec((map_count, ROWS_STEP, size), lambda i: (0, i, 0)),
-        ],
-        out_specs=pl.BlockSpec((stars, ROWS_STEP, size), lambda i: (0, i, 0)),
-        cost_estimate=pl.CostEstimate(
-            flops=2 * stars * ROWS_STEP * map_count * row_count * size,
-            bytes_accessed=2 * (map_count + stars) * row_count * size,
-            transcendentals=0,
-        ),
-        compiler_params=pltpu.CompilerParams(vmem_limit_bytes=24 << 20),
-        name="phase_turns",
-    )(inverse_wave, weights, feature_maps)
-
-
 def spread_rows(weights):
     eye = jnp.eye(ROWS_STEP, dtype=weights.dtype)
     outs, ins = weights.shape
     spread = weights[:, None, :, None] * eye[None, :, None, :]
     return spread.reshape(outs * ROWS_STEP, ins * ROWS_STEP)
-
-
-def star_kernel(
-    chunk, wave_ref, turns_ref, cot_ref, right_ref, left_ref, out_ref, pr, pi, yr, yi, ct, xr, xi
-):
-    size = turns_ref.shape[1]
-    quarter = size // RADIX
-    steps = size // chunk
-    blocks = [slice(m * quarter, (m + 1) * quarter) for m in range(RADIX)]
-    centre = 0.5 * (size - 1)
-    scale = 1.0 / size
-
-    def forward_columns(step, carry):
-        rows = pl.ds(pl.multiple_of(step * chunk, chunk), chunk)
-        cosine, sine = turn_cos_sin(turns_ref[rows, :].astype(F32))
-        row_pos = (
-            lax.broadcasted_iota(jnp.int32, (chunk, size), 0) + step * chunk
-        ).astype(F32) - centre
-        col_pos = lax.broadcasted_iota(jnp.int32, (chunk, size), 1).astype(F32) - centre
-        inside = row_pos * row_pos + col_pos * col_pos <= 0.25 * size * size
-        real = jnp.where(inside, cosine, 0.0)
-        imag = jnp.where(inside, sine, 0.0)
-        pr[rows, :] = real
-        pi[rows, :] = imag
-        mixed_real, mixed_imag = butterfly(
-            [real[:, b] for b in blocks], [imag[:, b] for b in blocks], -1
-        )
-        for k in range(RADIX):
-            both = jnp.concatenate([mixed_real[k].astype(BF16), mixed_imag[k].astype(BF16)], 1)
-            made = jnp.dot(both, right_ref[k], preferred_element_type=F32).astype(BF16)
-            yr[rows, blocks[k]] = made[:, :quarter]
-            yi[rows, blocks[k]] = made[:, quarter:]
-        return carry
-
-    lax.fori_loop(0, steps, forward_columns, 0)
-
-    def pick(k):
-        j = lax.broadcasted_iota(jnp.int32, (quarter, size), 0)
-        f = lax.broadcasted_iota(jnp.int32, (quarter, size), 1)
-        return jnp.where(f == RADIX * j + k, 1.0, 0.0).astype(BF16)
-
-    nt = (((1,), (1,)), ((), ()))
-    for k in range(RADIX):
-        part = lax.dot_general(
-            pick(k), cot_ref[...], nt, preferred_element_type=F32
-        ).astype(BF16)
-        for m in range(RADIX):
-            ct[blocks[k], blocks[m]] = lax.dot_general(
-                part, pick(m), nt, preferred_element_type=F32
-            )
-
-    def focal(step, carry):
-        cols = pl.ds(pl.multiple_of(step * quarter, quarter), quarter)
-        mixed_real, mixed_imag = butterfly(
-            [yr[b, cols].astype(F32) for b in blocks],
-            [yi[b, cols].astype(F32) for b in blocks],
-            -1,
-        )
-        back_real, back_imag = [], []
-        for k in range(RADIX):
-            both = jnp.concatenate([mixed_real[k].astype(BF16), mixed_imag[k].astype(BF16)], 0)
-            field = jnp.dot(left_ref[k], both, preferred_element_type=F32)
-            weight = ct[blocks[k], cols] * (2.0 * scale)
-            grad = (field * jnp.concatenate([weight, weight], 0)).astype(BF16)
-            back = jnp.dot(right_ref[k], grad, preferred_element_type=F32)
-            back_real.append(back[:quarter])
-            back_imag.append(back[quarter:])
-        spec_real, spec_imag = butterfly(back_real, back_imag, 1)
-        for m in range(RADIX):
-            xr[blocks[m], cols] = (spec_real[m] * scale).astype(BF16)
-            xi[blocks[m], cols] = (spec_imag[m] * scale).astype(BF16)
-        return carry
-
-    lax.fori_loop(0, RADIX, focal, 0)
-
-    def inverse_columns(step, carry):
-        rows = pl.ds(pl.multiple_of(step * chunk, chunk), chunk)
-        part_real, part_imag = [], []
-        for k in range(RADIX):
-            both = jnp.concatenate([xr[rows, blocks[k]], xi[rows, blocks[k]]], 1)
-            made = jnp.dot(both, left_ref[k], preferred_element_type=F32)
-            part_real.append(made[:, :quarter])
-            part_imag.append(made[:, quarter:])
-        grad_real, grad_imag = butterfly(part_real, part_imag, 1)
-        wave = wave_ref[0]
-        for m in range(RADIX):
-            grad = pr[rows, blocks[m]] * grad_imag[m] - pi[rows, blocks[m]] * grad_real[m]
-            out_ref[rows, blocks[m]] = (wave * grad).astype(BF16)
-        return carry
-
-    lax.fori_loop(0, steps, inverse_columns, 0)
-
-
-def star_gradient(wave, turns, cotangent, right, left):
-    size = turns.shape[0]
-    vmem = pl.BlockSpec(memory_space=pltpu.VMEM)
-    square = (size, size)
-    return pl.pallas_call(
-        functools.partial(star_kernel, 128),
-        out_shape=jax.ShapeDtypeStruct(square, BF16),
-        in_specs=[pl.BlockSpec(memory_space=pltpu.SMEM), vmem, vmem, vmem, vmem],
-        out_specs=vmem,
-        scratch_shapes=[
-            pltpu.VMEM(square, F32),
-            pltpu.VMEM(square, F32),
-            pltpu.VMEM(square, BF16),
-            pltpu.VMEM(square, BF16),
-            pltpu.VMEM(square, F32),
-            pltpu.VMEM(square, BF16),
-            pltpu.VMEM(square, BF16),
-        ],
-        compiler_params=pltpu.CompilerParams(vmem_limit_bytes=56 << 20),
-        name="star_gradient",
-    )(wave, turns, cotangent, right, left)
 
 
 def maps_kernel(group_ref, weight_ref, grad_ref, maps_ref, out_ref, score_ref):
@@ -409,112 +268,6 @@
         device_id=peer,
         device_id_type=pl.DeviceIdType.MESH,
     )
-
-
-DELIVER_STEPS = 4
-
-
-def deliver_kernel(
-    groups, lanes, pick_ref, turns_ref, cot_ref, turns_out, cot_out, stage, *scratch
-):
-    arrived, sems = scratch[:DELIVER_STEPS], scratch[DELIVER_STEPS:]
-    t_local, t_send, t_recv, s_local, s_send, s_recv, z_local, z_send, z_recv = sems
-    row = lax.axis_index("row")
-    me = lax.axis_index("star")
-    capacity = cot_ref.shape[1]
-    depth = cot_ref.shape[2] // DELIVER_STEPS
-    row_peers = [{"row": (row + d) % lanes} for d in range(1, lanes)]
-    star_peers = [{"star": (me + d) % groups} for d in range(1, groups)]
-    greet(row_peers + star_peers)
-    turns = [
-        send(
-            turns_ref.at[(row + d) % lanes],
-            turns_out.at[row],
-            t_send.at[d - 1],
-            t_recv.at[d - 1],
-            row_peers[d - 1],
-        )
-        for d in range(1, lanes)
-    ]
-    turns.append(pltpu.make_async_copy(turns_ref.at[row], turns_out.at[row], t_local))
-    for copy in turns:
-        copy.start()
-    steps = []
-    for step in range(DELIVER_STEPS):
-        rows = pl.ds(step * depth, depth)
-        target = arrived[step].at[pl.ds(me * capacity, capacity)]
-        copies = [
-            send(
-                cot_ref.at[(me + d) % groups, :, rows],
-                target,
-                s_send.at[step, d - 1],
-                s_recv.at[step, d - 1],
-                star_peers[d - 1],
-            )
-            for d in range(1, groups)
-        ]
-        copies.append(pltpu.make_async_copy(cot_ref.at[me, :, rows], target, s_local.at[step]))
-        for copy in copies:
-            copy.start()
-        steps.append(copies)
-    sent = []
-    for step in range(DELIVER_STEPS):
-        rows = pl.ds(step * depth, depth)
-        for copy in steps[step]:
-            copy.wait()
-        for lane in range(lanes):
-            stage[lane, rows] = arrived[step][pick_ref[lane]]
-        copies = [
-            send(
-                stage.at[(row + d) % lanes, rows],
-                cot_out.at[row, rows],
-                z_send.at[step, d - 1],
-                z_recv.at[step, d - 1],
-                row_peers[d - 1],
-            )
-            for d in range(1, lanes)
-        ]
-        copies.append(
-            pltpu.make_async_copy(stage.at[row, rows], cot_out.at[row, rows], z_local.at[step])
-        )
-        for copy in copies:
-            copy.start()
-        sent += copies
-    for copy in turns + sent:
-        copy.wait()
-
-
-def deliver(picks, turns, outgoing):
-    groups, capacity, row_count, size = outgoing.shape
-    lanes = turns.shape[0]
-    depth = row_count // DELIVER_STEPS
-    dma = pltpu.SemaphoreType.DMA
-    hbm = pl.BlockSpec(memory_space=pl.ANY)
-    vmem = pl.BlockSpec(memory_space=pltpu.VMEM)
-    shape = jax.ShapeDtypeStruct((lanes, row_count, size), BF16)
-    return pl.pallas_call(
-        functools.partial(deliver_kernel, groups, lanes),
-        out_shape=(shape, shape),
-        in_specs=[pl.BlockSpec(memory_space=pltpu.SMEM), vmem, hbm],
-        out_specs=(hbm, hbm),
-        scratch_shapes=[pltpu.VMEM((lanes, row_count, size), BF16)]
-        + [pltpu.VMEM((groups * capacity, depth, size), BF16)] * DELIVER_STEPS
-        + [
-            dma,
-            dma((lanes - 1,)),
-            dma((lanes - 1,)),
-            dma((DELIVER_STEPS,)),
-            dma((DELIVER_STEPS, groups - 1)),
-            dma((DELIVER_STEPS, groups - 1)),
-            dma((DELIVER_STEPS,)),
-            dma((DELIVER_STEPS, lanes - 1)),
-            dma((DELIVER_STEPS, lanes - 1)),
-        ],
-        compiler_params=pltpu.CompilerParams(
-            collective_id=0, has_side_effects=True, vmem_limit_bytes=56 << 20
-        ),
-        name="deliver",
-    )(picks, turns, outgoing)
 
 
 def gather_kernel(lanes, in_ref, out_ref, local, z_send, z_recv, p_send, p_recv, c_send, c_recv):
@@ -670,54 +423,476 @@
     )(scores)
 
 
+def plan_kernel(slots, count_ref, cell_ref, band_ref, cells_out, inverse_out, wave_out, route_out):
+    chips = count_ref.shape[0] // 2
+    over_x, over_y = OVER_X, OVER_Y
+    share = STARS_CHIP
+    first = [count_ref[2 * c] for c in range(chips)]
+    held = [first[c] + count_ref[2 * c + 1] for c in range(chips)]
+    level = []
+    for y in range(chips // 2):
+        both = held[2 * y] + held[2 * y + 1]
+        if y == 0:
+            level += [both // 2, both - both // 2]
+        else:
+            level += [2 * share - level[0], 2 * share - level[1]]
+    keep_x = [jnp.minimum(held[c], level[c]) for c in range(chips)]
+    keep_y = [jnp.minimum(level[c], share) for c in range(chips)]
+
+    def choose(values, index):
+        out = values[0]
+        for c in range(1, chips):
+            out = jnp.where(index == c, values[c], out)
+        return out
+
+    def slot_of(chip, place):
+        place = jnp.minimum(place, choose(held, chip) - 1)
+        start = choose(first, chip)
+        return jnp.where(place < start, place, slots + place - start)
+
+    def after_x(chip, place):
+        place = jnp.minimum(place, choose(level, chip) - 1)
+        kept = choose(keep_x, chip)
+        return jnp.where(place < kept, slot_of(chip, place), 2 * slots + place - kept)
+
+    def star_x(chip, place):
+        kept = choose(keep_x, chip)
+        other = chip + 1 - 2 * (chip % 2)
+        own = chip * 2 * slots + slot_of(chip, place)
+        far = other * 2 * slots + slot_of(other, choose(keep_x, other) + place - kept)
+        return jnp.where(place < kept, own, far)
+
+    per_chip = over_x + over_y + share
+
+    def fill(chip, carry):
+        base = chip * per_chip
+        kept_x, kept_y = choose(keep_x, chip), choose(keep_y, chip)
+        for i in range(over_x):
+            route_out[base + i] = slot_of(chip, kept_x + i)
+        for i in range(over_y):
+            route_out[base + over_x + i] = after_x(chip, kept_y + i)
+        other = chip + 2 - 4 * (chip // 2)
+        for i in range(share):
+            from_y = 2 * slots + over_x + i - kept_y
+            route_out[base + over_x + over_y + i] = jnp.where(
+                i < kept_y, after_x(chip, i), from_y
+            )
+            star = jnp.where(
+                i < kept_y, star_x(chip, i), star_x(other, choose(keep_y, other) + i - kept_y)
+            )
+            group = star // slots
+            band = band_ref[group, star - group * slots]
+            at = chip * share + i
+            cells_out[at] = cell_ref[group, star - group * slots]
+            inverse, wave = jnp.float32(0), jnp.float32(0)
+            for b in range(BANDS):
+                length = 0.55 + 0.35 * b / (BANDS - 1)
+                inverse = jnp.where(band == b, np.float32(1.0 / length), inverse)
+                wave = jnp.where(band == b, np.float32(2.0 * np.pi / length), wave)
+            inverse_out[at] = inverse
+            wave_out[at] = wave
+        return carry
+
+    lax.fori_loop(0, chips, fill, 0)
+
+
+def plan(star_counts, star_cells, star_bands):
+    smem = pl.BlockSpec(memory_space=pltpu.SMEM)
+    groups, slots = star_cells.shape
+    chips = groups // 2
+    total = chips * STARS_CHIP
+    return pl.pallas_call(
+        functools.partial(plan_kernel, slots),
+        out_shape=(
+            jax.ShapeDtypeStruct((total,), jnp.int32),
+            jax.ShapeDtypeStruct((total,), F32),
+            jax.ShapeDtypeStruct((total,), F32),
+            jax.ShapeDtypeStruct((chips * (OVER_X + OVER_Y + STARS_CHIP),), jnp.int32),
+        ),
+        in_specs=[smem] * 3,
+        out_specs=(smem,) * 4,
+        name="plan",
+    )(star_counts, star_cells, star_bands)
+
+
+def group_rows(step, depth, row_count, lanes):
+    return [
+        pl.ds(pl.multiple_of(lane * row_count + step * depth, depth), depth)
+        for lane in range(lanes)
+    ]
+
+
+def focal_kernel(
+    groups, lanes, cell_ref, inverse_ref, route_ref, coef_ref, maps_ref, cot_ref, right_ref, left_ref,
+    turns_out, xr, xi, maps_buf, stage, raw, pool, x_stage, y_stage, z_stage, ct, ct_turned,
+    order, spread, yr, yi, *scratch,
+):
+    steps = TURN_STEPS
+    chunks = pool.shape[0]
+    x_got, y_got = scratch[:chunks], scratch[chunks : 2 * chunks]
+    (
+        m_sem, t_local, t_send, t_recv, r_local, r_send, r_recv, x_send, x_recv,
+        y_send, y_recv, z_local, z_send, z_recv,
+    ) = scratch[2 * chunks :]
+    row = lax.axis_index("row")
+    me = lax.axis_index("star")
+    core = me % 2
+    chip = me // 2
+    twin = me + 1 - 2 * core
+    over_x = me + 2 - 4 * (chip % 2)
+    over_y = me + 4 - 8 * (me // 4)
+    map_count, depth, size = maps_buf.shape[1:]
+    row_count = depth * steps
+    half = size // 2
+    quarter = size // RADIX
+    slots = raw.shape[0] // 2
+    places = [(d, e) for e in range(2) for d in range(lanes)][1:]
+    peers = [{"row": (row + d) % lanes, "star": twin if e else me} for d, e in places]
+    greet(peers + [{"star": over_x}, {"star": over_y}])
+
+    slot_range = pl.ds(core * slots, slots)
+    other = 1 - core
+    raw_own = pltpu.make_async_copy(
+        cot_ref.at[:, :, pl.ds(pl.multiple_of(core * half, half), half)], raw.at[slot_range], r_local
+    )
+    raw_twin = send(
+        cot_ref.at[:, :, pl.ds(pl.multiple_of(other * half, half), half)],
+        raw.at[slot_range],
+        r_send,
+        r_recv,
+        {"star": twin},
+    )
+    raw_own.start()
+    raw_twin.start()
+
+    def fetch(step):
+        slot = step % 2
+        rows = pl.ds(pl.multiple_of(step * depth, depth), depth)
+        return pltpu.make_async_copy(maps_ref.at[:, rows], maps_buf.at[slot], m_sem.at[slot])
+
+    fetch(0).start()
+    fetch(1).start()
+
+    lines = lanes * ROWS_STEP
+    wide = map_count * ROWS_STEP
+    cells = lax.broadcasted_iota(jnp.int32, (ROWS_STEP, coef_ref.shape[0]), 1)
+    hot = jnp.concatenate(
+        [
+            jnp.where(cells == cell_ref[me * lanes + s], 1.0, 0.0).astype(BF16)
+            for s in range(lanes)
+        ],
+        0,
+    )
+    coefs = jnp.dot(hot, coef_ref[...], preferred_element_type=F32).astype(BF16)
+    at = lax.broadcasted_iota(jnp.int32, (map_count, wide), 0)
+    to = lax.broadcasted_iota(jnp.int32, (map_count, wide), 1)
+    repeat = jnp.where(to // ROWS_STEP == at, 1.0, 0.0).astype(BF16)
+    repeated = jnp.dot(coefs, repeat, preferred_element_type=F32)
+    at = lax.broadcasted_iota(jnp.int32, (lines, wide), 0)
+    to = lax.broadcasted_iota(jnp.int32, (lines, wide), 1)
+    spread[...] = jnp.where(at % ROWS_STEP == to % ROWS_STEP, repeated, 0.0).astype(BF16)
+
+    def turn_copies(step):
+        rows = pl.ds(pl.multiple_of(step * depth, depth), depth)
+        place = pl.ds(pl.multiple_of(row * row_count + step * depth, depth), depth)
+        return [
+            pltpu.make_async_copy(stage.at[row, rows], turns_out.at[place], t_local.at[step])
+        ] + [
+            send(
+                stage.at[(row + d) % lanes, rows],
+                turns_out.at[place],
+                t_send.at[step, d - 1],
+                t_recv.at[step, d - 1],
+                {"row": (row + d) % lanes},
+            )
+            for d in range(1, lanes)
+        ]
+
+    def phase_step(step, carry):
+        slot = step % 2
+        fetch(step).wait()
+        for part in range(depth // ROWS_STEP):
+            lined = pl.ds(part * ROWS_STEP, ROWS_STEP)
+            maps = maps_buf[slot, :, lined].reshape(wide, size)
+            path = jnp.dot(spread[...], maps, preferred_element_type=F32)
+            rows = pl.ds(pl.multiple_of(step * depth + part * ROWS_STEP, ROWS_STEP), ROWS_STEP)
+            for s in range(lanes):
+                turned = path[s * ROWS_STEP : (s + 1) * ROWS_STEP] * inverse_ref[me * lanes + s]
+                stage[s, rows] = (turned - jnp.floor(turned + 0.5)).astype(BF16)
+        for copy in turn_copies(step):
+            copy.start()
+
+        @pl.when(step + 2 < steps)
+        def _():
+            fetch(step + 2).start()
+
+        return carry
+
+    lax.fori_loop(0, EARLY_STEPS, phase_step, 0)
+
+    def x_copy(c):
+        return send(x_stage.at[c], x_got[c], x_send.at[c], x_recv.at[c], {"star": over_x})
+
+    def y_copy(c):
+        return send(y_stage.at[c], y_got[c], y_send.at[c], y_recv.at[c], {"star": over_y})
+
+    tall = quarter // lanes
+    piece = tall * RADIX // chunks
+    parts = chunks // RADIX
+    per_chip = OVER_X + OVER_Y + STARS_CHIP
+    base = chip * per_chip
+
+    def z_copies(c):
+        kind, part = c // parts, c % parts
+        target = ct.at[
+            kind,
+            pl.ds(pl.multiple_of(row * tall + part * piece, piece), piece),
+            pl.ds(pl.multiple_of(core * half, half), half),
+        ]
+        own = z_stage.at[c, core * lanes + row]
+        return [pltpu.make_async_copy(own, target, z_local.at[c])] + [
+            send(
+                z_stage.at[c, (core + e) % 2 * lanes + (row + d) % lanes],
+                target,
+                z_send.at[c, n],
+                z_recv.at[c, n],
+                peers[n],
+            )
+            for n, (d, e) in enumerate(places)
+        ]
+
+    raw_own.wait()
+    raw_twin.wait()
+    at = lax.broadcasted_iota(jnp.int32, (row_count, row_count), 0)
+    to = lax.broadcasted_iota(jnp.int32, (row_count, row_count), 1)
+    sort = jnp.where(at % tall * RADIX + at // tall == to, 1.0, 0.0).astype(BF16)
+
+    def sort_slot(slot, carry):
+        sorted_rows = jnp.dot(sort, raw[slot], preferred_element_type=F32).astype(BF16)
+        for c in range(chunks):
+            pool[c, slot] = sorted_rows[c * piece : (c + 1) * piece]
+        return carry
+
+    lax.fori_loop(0, 2 * slots, sort_slot, 0)
+    for c in range(chunks):
+        for i in range(OVER_X):
+            x_stage[c, i] = pool[c, route_ref[base + i]]
+        x_copy(c).start()
+
+    lax.fori_loop(EARLY_STEPS, steps, phase_step, 0)
+    at = lax.broadcasted_iota(jnp.int32, (size, size), 0)
+    to = lax.broadcasted_iota(jnp.int32, (size, size), 1)
+    order[...] = jnp.where(at % quarter * RADIX + at // quarter == to, 1.0, 0.0).astype(BF16)
+
+    def pick_x(c, index):
+        mine = pool[c, jnp.minimum(index, 2 * slots - 1)]
+        far = x_got[c][jnp.clip(index - 2 * slots, 0, OVER_X - 1)]
+        return jnp.where(index < 2 * slots, mine, far)
+
+    def route(c):
+        x_copy(c).wait()
+        for i in range(OVER_Y):
+            y_stage[c, i] = pick_x(c, route_ref[base + OVER_X + i])
+        y_copy(c).start()
+        y_copy(c).wait()
+        for i in range(STARS_CHIP):
+            index = route_ref[base + OVER_X + OVER_Y + i]
+            far = y_got[c][jnp.clip(index - 2 * slots - OVER_X, 0, OVER_Y - 1)]
+            near = pick_x(c, jnp.minimum(index, 2 * slots + OVER_X - 1))
+            z_stage[c, i] = jnp.where(index < 2 * slots + OVER_X, near, far)
+        for copy in z_copies(c):
+            copy.start()
+
+    for c in range(chunks // 2):
+        route(c)
+
+    blocks = [slice(m * quarter, (m + 1) * quarter) for m in range(RADIX)]
+    centre = 0.5 * (size - 1)
+    scale = 1.0 / size
+    tile = lanes * depth
+
+    def forward_columns(step, carry):
+        for copy in turn_copies(step):
+            copy.wait()
+        rows = group_rows(step, depth, row_count, lanes)
+        turns = jnp.concatenate([turns_out[r, :] for r in rows], 0)
+        cosine, sine = turn_cos_sin(turns.astype(F32))
+        line = lax.broadcasted_iota(jnp.int32, (tile, size), 0)
+        place = line // depth * row_count + line % depth + step * depth
+        row_pos = place.astype(F32) - centre
+        col_pos = lax.broadcasted_iota(jnp.int32, (tile, size), 1).astype(F32) - centre
+        inside = row_pos * row_pos + col_pos * col_pos <= 0.25 * size * size
+        real = jnp.where(inside, cosine, 0.0)
+        imag = jnp.where(inside, sine, 0.0)
+        mixed_real, mixed_imag = butterfly(
+            [real[:, b] for b in blocks], [imag[:, b] for b in blocks], -1
+        )
+        for k in range(RADIX):
+            both = jnp.concatenate([mixed_real[k].astype(BF16), mixed_imag[k].astype(BF16)], 1)
+            made = jnp.dot(both, right_ref[k], preferred_element_type=F32).astype(BF16)
+            for lane in range(lanes):
+                lined = slice(lane * depth, (lane + 1) * depth)
+                yr[rows[lane], blocks[k]] = made[lined, :quarter]
+                yi[rows[lane], blocks[k]] = made[lined, quarter:]
+        return carry
+
+    lax.fori_loop(0, steps, forward_columns, 0)
+    for c in range(chunks // 2, chunks):
+        route(c)
+
+    def focal(kind, carry):
+        for part in range(parts):
+            for copy in z_copies(kind * parts + part):
+                copy.wait()
+        ct_turned[...] = lax.dot_general(
+            order[...], ct[kind], (((1,), (1,)), ((), ())), preferred_element_type=F32
+        )
+        cols = pl.ds(pl.multiple_of(kind * quarter, quarter), quarter)
+        mixed_real, mixed_imag = butterfly(
+            [yr[b, cols].astype(F32) for b in blocks],
+            [yi[b, cols].astype(F32) for b in blocks],
+            -1,
+        )
+        back_real, back_imag = [], []
+        for k in range(RADIX):
+            both = jnp.concatenate([mixed_real[k].astype(BF16), mixed_imag[k].astype(BF16)], 0)
+            field = jnp.dot(left_ref[k], both, preferred_element_type=F32)
+            weight = ct_turned[blocks[k], :] * (2.0 * scale)
+            grad = (field * jnp.concatenate([weight, weight], 0)).astype(BF16)
+            back = jnp.dot(right_ref[k], grad, preferred_element_type=F32)
+            back_real.append(back[:quarter])
+            back_imag.append(back[quarter:])
+        spec_real, spec_imag = butterfly(back_real, back_imag, 1)
+        for m in range(RADIX):
+            xr[blocks[m], cols] = (spec_real[m] * scale).astype(BF16)
+            xi[blocks[m], cols] = (spec_imag[m] * scale).astype(BF16)
+        return carry
+
+    lax.fori_loop(0, RADIX, focal, 0)
+
+
+def focal_fields(cells, inverse, route, coef_table, feature_maps, cotangent, right, left, groups, lanes):
+    map_count, row_count, size = feature_maps.shape
+    slots = cotangent.shape[0]
+    depth = row_count // TURN_STEPS
+    half, quarter = size // 2, size // RADIX
+    chunks = ROUTE_CHUNKS
+    piece = row_count // chunks
+    dma = pltpu.SemaphoreType.DMA
+    smem = pl.BlockSpec(memory_space=pltpu.SMEM)
+    vmem = pl.BlockSpec(memory_space=pltpu.VMEM)
+    hbm = pl.BlockSpec(memory_space=pl.ANY)
+    square = jax.ShapeDtypeStruct((size, size), BF16)
+    others = 2 * lanes - 1
+    return pl.pallas_call(
+        functools.partial(focal_kernel, groups, lanes),
+        out_shape=(square,) * 3,
+        in_specs=[smem, smem, smem, vmem, hbm, hbm, vmem, vmem],
+        out_specs=(vmem,) * 3,
+        scratch_shapes=[
+            pltpu.VMEM((2, map_count, depth, size), BF16),
+            pltpu.VMEM((lanes, row_count, size), BF16),
+            pltpu.VMEM((2 * slots, row_count, half), BF16),
+            pltpu.VMEM((chunks, 2 * slots, piece, half), BF16),
+            pltpu.VMEM((chunks, OVER_X, piece, half), BF16),
+            pltpu.VMEM((chunks, OVER_Y, piece, half), BF16),
+            pltpu.VMEM((chunks, STARS_CHIP, piece, half), BF16),
+            pltpu.VMEM((RADIX, quarter, size), BF16),
+            pltpu.VMEM((size, quarter), F32),
+            pltpu.VMEM((size, size), BF16),
+            pltpu.VMEM((lanes * ROWS_STEP, map_count * ROWS_STEP), BF16),
+            pltpu.VMEM((size, size), BF16),
+            pltpu.VMEM((size, size), BF16),
+        ]
+        + [pltpu.VMEM((OVER_X, piece, half), BF16)] * chunks
+        + [pltpu.VMEM((OVER_Y, piece, half), BF16)] * chunks
+        + [
+            dma((2,)),
+            dma((TURN_STEPS,)),
+            dma((TURN_STEPS, lanes - 1)),
+            dma((TURN_STEPS, lanes - 1)),
+            dma,
+            dma,
+            dma,
+            dma((chunks,)),
+            dma((chunks,)),
+            dma((chunks,)),
+            dma((chunks,)),
+            dma((chunks,)),
+            dma((chunks, others)),
+            dma((chunks, others)),
+        ],
+        compiler_params=pltpu.CompilerParams(
+            collective_id=0, has_side_effects=True, vmem_limit_bytes=60 << 20
+        ),
+        name="focal_fields",
+    )(cells, inverse, route, coef_table, feature_maps, cotangent, right, left)
+
+
+def column_kernel(chunk, wave_ref, turns_ref, xr, xi, left_ref, out_ref):
+    size = turns_ref.shape[1]
+    quarter = size // RADIX
+    blocks = [slice(m * quarter, (m + 1) * quarter) for m in range(RADIX)]
+    centre = 0.5 * (size - 1)
+
+    def inverse_columns(step, carry):
+        rows = pl.ds(pl.multiple_of(step * chunk, chunk), chunk)
+        cosine, sine = turn_cos_sin(turns_ref[rows, :].astype(F32))
+        row_pos = (
+            lax.broadcasted_iota(jnp.int32, (chunk, size), 0) + step * chunk
+        ).astype(F32) - centre
+        col_pos = lax.broadcasted_iota(jnp.int32, (chunk, size), 1).astype(F32) - centre
+        inside = row_pos * row_pos + col_pos * col_pos <= 0.25 * size * size
+        real = jnp.where(inside, cosine, 0.0)
+        imag = jnp.where(inside, sine, 0.0)
+        part_real, part_imag = [], []
+        for k in range(RADIX):
+            both = jnp.concatenate([xr[rows, blocks[k]], xi[rows, blocks[k]]], 1)
+            made = jnp.dot(both, left_ref[k], preferred_element_type=F32)
+            part_real.append(made[:, :quarter])
+            part_imag.append(made[:, quarter:])
+        grad_real, grad_imag = butterfly(part_real, part_imag, 1)
+        wave = wave_ref[0]
+        for m in range(RADIX):
+            grad = real[:, blocks[m]] * grad_imag[m] - imag[:, blocks[m]] * grad_real[m]
+            out_ref[rows, blocks[m]] = (wave * grad).astype(BF16)
+        return carry
+
+    lax.fori_loop(0, size // chunk, inverse_columns, 0)
+
+
+def column_gradient(wave, turns, spec_real, spec_imag, left):
+    vmem = pl.BlockSpec(memory_space=pltpu.VMEM)
+    return pl.pallas_call(
+        functools.partial(column_kernel, 128),
+        out_shape=jax.ShapeDtypeStruct(turns.shape, BF16),
+        in_specs=[pl.BlockSpec(memory_space=pltpu.SMEM), vmem, vmem, vmem, vmem],
+        out_specs=vmem,
+        compiler_params=pltpu.CompilerParams(vmem_limit_bytes=56 << 20),
+        name="column_gradient",
+    )(wave, turns, spec_real, spec_imag, left)
+
+
 def star_devices(feature_maps, coef_table, star_counts, star_cells, star_bands, psf_cotangent):
     groups = lax.axis_size("star")
     lanes = lax.axis_size("row")
     my_group = lax.axis_index("star")
     my_lane = lax.axis_index("row")
-    slot_count = psf_cotangent.shape[0]
     map_count, row_count, size = feature_maps.shape
     cell_count = coef_table.shape[0]
     share = map_count // groups
-    group_ends = jnp.cumsum(star_counts)
-    group_starts = group_ends - star_counts
-    capacity = -(-slot_count // groups)
-    targets = jnp.arange(groups, dtype=jnp.int32)
-    my_start = table_pick(group_starts, my_group[None])
-    first_slot = (targets - my_start) % groups
-    lane_index = jnp.arange(capacity, dtype=jnp.int32)
-    send_slot = (first_slot[:, None] + lane_index[None, :] * groups).reshape(-1)
-    outgoing = jnp.take(
-        psf_cotangent, jnp.minimum(send_slot, slot_count - 1), axis=0, mode="clip"
-    )
-    outgoing = outgoing.reshape((groups, capacity) + outgoing.shape[1:])
-
     total = groups * lanes
-    order = jnp.arange(total, dtype=jnp.int32)
-    rank = order // lanes + (order % lanes) * groups
-    owner = jnp.sum((group_ends[None, :] <= rank[:, None]).astype(jnp.int32), axis=1)
-    within = rank - table_pick(group_starts, owner)
-    slot_index = owner * slot_count + within
-    cell_ids = table_pick(star_cells.reshape(-1), slot_index)
-    band_ids = table_pick(star_bands.reshape(-1), slot_index)
+    cell_ids, inverse, wave, route = plan(star_counts, star_cells, star_bands)
     cell_hot = cell_ids[:, None] == jnp.arange(cell_count, dtype=jnp.int32)[None, :]
     coef_rows = jnp.dot(
         cell_hot.astype(BF16), coef_table, preferred_element_type=F32
     ).astype(BF16)
-
-    def mine(values):
-        return lax.dynamic_slice_in_dim(values, my_group * lanes, lanes, 0)
-
-    wavelength = 0.55 + 0.35 * band_ids.astype(F32) / (BANDS - 1)
-    turns = phase_turns(mine(1.0 / wavelength), mine(coef_rows), feature_maps)
-    picks = mine(owner) * capacity + mine(within) // groups
-    turns, cotangent = deliver(picks, turns, outgoing)
-    wave = wave_numbers(band_ids)
+    right, left = quarter_tables(size)
+    turns, spec_real, spec_imag = focal_fields(
+        cell_ids, inverse, route, coef_table, feature_maps, psf_cotangent, right, left, groups, lanes
+    )
     my_wave = lax.dynamic_slice_in_dim(wave, my_group * lanes + my_lane, 1, 0)
-    right, left = quarter_tables(size)
-    path_grad = star_gradient(
-        my_wave, turns.reshape(size, size), cotangent.reshape(size, size), right, left
-    )
+    path_grad = column_gradient(my_wave, turns, spec_real, spec_imag, left)
     path_grads = gather_grads(path_grad.reshape(lanes, row_count, size), groups)
     path_grads = path_grads.reshape(total, row_count, size)
     my_coefs = lax.dynamic_slice_in_dim(coef_rows.T, my_group * share, share, 0)

time: 303 us -> 254 us (0.84)
  Pallas kernels: 275 us -> 241 us
  local copies, waits for them, and re-layouts: 17.5 us -> 5.52 us
  other arithmetic: 4.47 us -> 0.49 us
    pallas_call x3, Pallas kernels: 157 us -> 124 us  [the longest x1 107 us: focal_fields(): pl.pallas_call(functools.partial(focal_kernel, groups, lanes), out_shape=...]
    gather x1 -> x0, local copies, waits for them, and re-layouts: 7.69 us -> none  [star_devices(): jnp.take(psf_cotangent, jnp.minimum(send_slot, slot_count - 1), axis=0, m...]
where the time goes in v1:
time: 254 us; the launch traced here: 249 us
  Pallas kernels  241 us (95%)
  local copies, waits for them, and re-layouts  5.52 us (2%)
    pallas_call x1, Pallas kernels, focal_fields(): pl.pallas_call(functools.partial(focal_kernel, groups, lanes), out_shape=...  107 us
    pallas_call x1, Pallas kernels, gather_grads(): pl.pallas_call(functools.partial(gather_kernel, lanes), out_shape=jax.Sha...  84.8 us
    pallas_call x1, Pallas kernels, map_sums(): pl.pallas_call(maps_kernel, out_shape=(jax.ShapeDtypeStruct((share, row_c...  20.4 us
    pallas_call x1, Pallas kernels, column_gradient(): pl.pallas_call(functools.partial(column_kernel, 128), out_shape=jax.Shape...  14.2 us
    pallas_call x1, Pallas kernels, gather_scores(): pl.pallas_call(functools.partial(score_kernel, groups, lanes), out_shape=...  12 us

profile of v1, /device:TPU:27, one launch (start us, length us, event | category | flops | bytes accessed | tf_op | source)
XLA Modules:
  0.0 249.2 jit_solution(8743522034336911966)
XLA Ops:
  0.6 2.9 %plan.1 = (s32[32]{0:T(128)}, f32[32]{0:T(128)}, f32[32]{0:T(128)}, s32[100]{0:T(128)}) custom-call(s32[8]{0:T(128)} %count_ref.1, s32[8,12]{1,0:T(8,128)} %cell_ref.1, s32[8,12]{1,0:T(8,128)} %band_ref.1), custom_call_target="tpu_custom_call" | custom-call | tf_op jit(solution)/shard_map/plan/pallas_call | solution.py:504
  3.5 1.3 dynamic_slice.7.wave_ref
  4.8 107.2 %focal_fields.1 = (bf16[1024,1024]{1,0:T(8,128)(2,1)}, bf16[1024,1024]{1,0:T(8,128)(2,1)}, bf16[1024,1024]{1,0:T(8,128)(2,1)}) custom-call(s32[32]{0:T(128)} %get-tuple-element.11.cell_ref, f32[32]{0:T(128)} %get-tuple-element.13.inverse_ref, s32[100]{0:T(128)} %get-tuple-element.14.route_ref, bf16[64,64]{1,0:T(8,128)(2,1)} %coef_ref.1, ...), custom_call_target="tpu_custom_call" | custom-call | tf_op jit(solution)/shard_map/focal_fields/pallas_call | solution.py:787
  112.0 14.2 %column_gradient.1 = bf16[1024,1024]{1,0:T(8,128)(2,1)} custom-call(f32[1]{0:T(128)} %dynamic_slice.7.wave_ref, bf16[1024,1024]{1,0:T(8,128)(2,1)} %get-tuple-element.15.turns_ref, bf16[1024,1024]{1,0:T(8,128)(2,1)} %get-tuple-element.16.xr, bf16[1024,1024]{1,0:T(8,128)(2,1)} %get-tuple-element.17.xi, bf16[4,512,512]{2,1,0:T(8,128)(2,1)} %constant.29.clone.left_ref), custom_call_target="tpu_custom_call" | custom-call | tf_op jit(solution)/shard_map/column_gradient/pallas_call | solution.py:866
  126.2 0.0 copy-start
  126.2 0.0 copy-start.1
  126.2 84.8 %gather_grads.1 = bf16[8,4,256,1024]{3,2,1,0:T(8,128)(2,1)} custom-call(bf16[4,256,1024]{2,1,0:T(8,128)(2,1)} %bitcast.10), custom_call_target="tpu_custom_call" | custom-call | tf_op jit(solution)/shard_map/gather_grads/pallas_call | solution.py:359
  211.0 0.0 copy-done
  211.0 0.0 copy-done.1
  211.0 0.2 fusion.3
  211.2 0.1 broadcast_multiply_fusion
  211.4 2.5 mul.41.weight_ref
  213.8 20.4 %map_sums.1 = (f32[8,256,1024]{2,1,0:T(8,128)}, f32[128,512]{1,0:T(8,128)}) custom-call(s32[1]{0:T(128)} %bitcast.group_ref, bf16[128,512]{1,0:T(8,128)(2,1)} %mul.41.weight_ref, bf16[32,256,1024]{2,1,0:T(8,128)(2,1)} %bitcast.9, bf16[64,256,1024]{2,1,0:T(8,128)(2,1)} %maps_ref.3), custom_call_target="tpu_custom_call" | custom-call | tf_op jit(solution)/shard_map/map_sums/pallas_call | solution.py:225
  234.2 1.7 reshape.37
  236.0 0.3 multiply_reduce_fusion
  236.3 12.0 %gather_scores.1 = f32[8,4,8,128]{3,2,1,0:T(8,128)S(1)} custom-call(f32[8,128]{1,0:T(8,128)S(1)} %pad.4.in_ref), custom_call_target="tpu_custom_call" | custom-call | tf_op jit(solution)/shard_map/gather_scores/pallas_call | solution.py:408
  248.4 0.9 fusion
  (5 shorter events, 0.0 us)
Async XLA Ops:
  126.2 84.8 %copy-start = (bf16[64,64]{1,0:T(8,128)(2,1)S(1)}, bf16[64,64]{1,0:T(8,128)(2,1)}, u32[]{:S(2)}) copy-start(bf16[64,64]{1,0:T(8,128)(2,1)} %coef_ref.1) | copy-start | bytes 24580
  126.2 84.8 %copy-start.1 = (s32[32]{0:T(128)S(1)}, s32[32]{0:T(128)}, u32[]{:S(2)}) copy-start(s32[32]{0:T(128)} %get-tuple-element.11.cell_ref) | copy-start | bytes 388

commit v2 on v1

--- a/solution.py
+++ b/solution.py
@@ -16,6 +16,7 @@
 TURN_STEPS = 8
 EARLY_STEPS = 2
 ROUTE_CHUNKS = 8
+GATHER_STEPS = 8
 OVER_X = 11
 OVER_Y = 6
 STARS_CHIP = 8
@@ -156,17 +157,18 @@
     return (map_grad.reshape(share, row_count, pupil_size), coef_grad)
 
 
-def quarter_tables(size):
+def half_tables(size):
     quarter = size // RADIX
     place = np.arange(quarter)[None, :, None]
     freq = RADIX * np.arange(quarter)[None, None, :] + np.arange(RADIX)[:, None, None]
     angle = 2.0 * np.pi / size * ((place * freq) % size)
     cosine, sine = np.cos(angle), -np.sin(angle)
-    right = np.concatenate(
-        [np.concatenate([cosine, sine], 2), np.concatenate([-sine, cosine], 2)], 1
-    ).astype(np.float32)
-    left = np.swapaxes(right, 1, 2)
-    return jnp.asarray(right.astype(jnp.bfloat16)), jnp.asarray(left.astype(jnp.bfloat16))
+    right = np.concatenate([cosine, sine], 2).astype(np.float32)
+    left = np.concatenate([np.swapaxes(cosine, 1, 2), np.swapaxes(sine, 1, 2)], 2)
+    return (
+        jnp.asarray(right.astype(jnp.bfloat16)),
+        jnp.asarray(left.astype(np.float32).astype(jnp.bfloat16)),
+    )
 
 
 def turn_cos_sin(turns):
@@ -195,63 +197,6 @@
     )
 
 
-def spread_rows(weights):
-    eye = jnp.eye(ROWS_STEP, dtype=weights.dtype)
-    outs, ins = weights.shape
-    spread = weights[:, None, :, None] * eye[None, :, None, :]
-    return spread.reshape(outs * ROWS_STEP, ins * ROWS_STEP)
-
-
-def maps_kernel(group_ref, weight_ref, grad_ref, maps_ref, out_ref, score_ref):
-    share, rows, size = out_ref.shape
-    grads = grad_ref[...].reshape(grad_ref.shape[0] * rows, size)
-    maps = maps_ref[...].reshape(share * rows, size)
-    total = jnp.dot(weight_ref[...], grads, preferred_element_type=F32)
-    out_ref[...] = total.reshape(share, rows, size)
-
-    @pl.when(pl.program_id(0) == 0)
-    def _():
-        score_ref[...] = jnp.zeros_like(score_ref)
-
-    score_ref[...] += lax.dot_general(
-        maps, grads, (((1,), (1,)), ((), ())), preferred_element_type=F32
-    )
-
-
-def map_sums(my_group, coef_rows, path_grads, feature_maps, share):
-    stars, row_count, size = path_grads.shape
-    weights = spread_rows(coef_rows)
-    score_shape = (share * ROWS_STEP, stars * ROWS_STEP)
-    map_grad, scores = pl.pallas_call(
-        maps_kernel,
-        out_shape=(
-            jax.ShapeDtypeStruct((share, row_count, size), F32),
-            jax.ShapeDtypeStruct(score_shape, F32),
-        ),
-        grid_spec=pltpu.PrefetchScalarGridSpec(
-            num_scalar_prefetch=1,
-            grid=(row_count // ROWS_STEP,),
-            in_specs=[
-                pl.BlockSpec(weights.shape, lambda i, g: (0, 0)),
-                pl.BlockSpec((stars, ROWS_STEP, size), lambda i, g: (0, i, 0)),
-                pl.BlockSpec((share, ROWS_STEP, size), lambda i, g: (g[0], i, 0)),
-            ],
-            out_specs=(
-                pl.BlockSpec((share, ROWS_STEP, size), lambda i, g: (0, i, 0)),
-                pl.BlockSpec(score_shape, lambda i, g: (0, 0)),
-            ),
-        ),
-        compiler_params=pltpu.CompilerParams(vmem_limit_bytes=56 << 20),
-        name="map_sums",
-    )(my_group[None], weights, path_grads, feature_maps)
-    eye = jnp.eye(ROWS_STEP, dtype=F32)
-    scores = scores.reshape(share, ROWS_STEP, stars, ROWS_STEP)
-    return map_grad, jnp.sum(scores * eye[None, :, None, :], axis=(1, 3))
-
-
-GATHER_STEPS = 8
-
-
 def greet(peers):
     barrier = pltpu.get_barrier_semaphore()
     for peer in peers:
@@ -270,157 +215,15 @@
     )
 
 
-def gather_kernel(lanes, in_ref, out_ref, local, z_send, z_recv, p_send, p_recv, c_send, c_recv):
-    row = lax.axis_index("row")
-    me = lax.axis_index("star")
-    depth = in_ref.shape[1] // GATHER_STEPS
-    core = me + 1 - 2 * (me % 2)
-    across = me + 2 - 4 * ((me // 2) % 2)
-    along = me + 4 - 8 * ((me // 4) % 2)
-    corner = across + 4 - 8 * ((me // 4) % 2)
-    peers = [{"row": (row + d) % lanes} for d in range(1, lanes)]
-    to_core, to_across, to_along = {"star": core}, {"star": across}, {"star": along}
-    greet(peers + [to_core, to_across, to_along])
-    half = lanes // 2
-    started = []
-
-    def start(copy):
-        copy.start()
-        started.append(copy)
-        return copy
-
-    def block(group, step, first=0, count=lanes):
-        return out_ref.at[group, pl.ds(first, count), pl.ds(step * depth, depth)]
-
-    own, exchanged = [], []
-    for step in range(GATHER_STEPS):
-        rows = pl.ds(step * depth, depth)
-        copy = pltpu.make_async_copy(
-            in_ref.at[row, rows], out_ref.at[me, row, rows], local.at[step]
-        )
-        copy.start()
-        own.append(copy)
-        exchanged.append(
-            [
-                start(
-                    send(
-                        in_ref.at[(row + d) % lanes, rows],
-                        out_ref.at[me, row, rows],
-                        z_send.at[step, d - 1],
-                        z_recv.at[step, d - 1],
-                        peers[d - 1],
-                    )
-                )
-                for d in range(1, lanes)
-            ]
-        )
-
-    def plane(step, way, part, peer):
-        return start(send(part, part, p_send.at[step, way], p_recv.at[step, way], peer))
-
-    def cores(step, way, part):
-        return start(send(part, part, c_send.at[step, way], c_recv.at[step, way], to_core))
-
-    sides, corners, twins = {}, {}, []
-    for step in range(GATHER_STEPS + 2):
-        if step < GATHER_STEPS:
-            own[step].wait()
-            for copy in exchanged[step]:
-                copy.wait_recv()
-            part = block(me, step)
-            sides[step] = (
-                plane(step, 0, part, to_across),
-                plane(step, 1, part, to_along),
-            )
-            twins.append(cores(step, 0, part))
-        last = step - 1
-        if 0 <= last < GATHER_STEPS:
-            sides[last][0].wait_recv()
-            first = plane(last, 2, block(across, last, 0, half), to_along)
-            twins.append(cores(last, 1, block(across, last)))
-            sides[last][1].wait_recv()
-            second = plane(last, 3, block(along, last, half, lanes - half), to_across)
-            twins.append(cores(last, 2, block(along, last)))
-            corners[last] = (first, second)
-        last = step - 2
-        if last >= 0:
-            corners[last][0].wait_recv()
-            corners[last][1].wait_recv()
-            twins.append(cores(last, 3, block(corner, last)))
-    for copy in twins:
-        copy.wait_recv()
-    for copy in started:
-        copy.wait_send()
-
-
-def gather_grads(path_grad, groups):
-    lanes, row_count, size = path_grad.shape
-    dma = pltpu.SemaphoreType.DMA
-    return pl.pallas_call(
-        functools.partial(gather_kernel, lanes),
-        out_shape=jax.ShapeDtypeStruct((groups, lanes, row_count, size), path_grad.dtype),
-        in_specs=[pl.BlockSpec(memory_space=pltpu.VMEM)],
-        out_specs=pl.BlockSpec(memory_space=pl.ANY),
-        scratch_shapes=[
-            dma((GATHER_STEPS,)),
-            dma((GATHER_STEPS, lanes - 1)),
-            dma((GATHER_STEPS, lanes - 1)),
-            dma((GATHER_STEPS, 4)),
-            dma((GATHER_STEPS, 4)),
-            dma((GATHER_STEPS, 4)),
-            dma((GATHER_STEPS, 4)),
-        ],
-        compiler_params=pltpu.CompilerParams(
-            collective_id=1, has_side_effects=True, vmem_limit_bytes=56 << 20
-        ),
-        name="gather_grads",
-    )(path_grad)
-
-
-def score_kernel(groups, lanes, in_ref, out_ref, z_send, z_recv, s_send, s_recv):
-    row = lax.axis_index("row")
-    me = lax.axis_index("star")
-    row_peers = [{"row": (row + d) % lanes} for d in range(1, lanes)]
-    star_peers = [{"star": (me + d) % groups} for d in range(1, groups)]
-    greet(row_peers + star_peers)
-    copies = [
-        send(in_ref, out_ref.at[me, row], z_send.at[d], z_recv.at[d], row_peers[d])
-        for d in range(lanes - 1)
-    ]
-    for copy in copies:
-        copy.start()
-    out_ref[me, row] = in_ref[...]
-    for copy in copies:
-        copy.wait()
-    copies = [
-        send(out_ref.at[me], out_ref.at[me], s_send.at[d], s_recv.at[d], star_peers[d])
-        for d in range(groups - 1)
-    ]
-    for copy in copies:
-        copy.start()
-    for copy in copies:
-        copy.wait()
-
-
-def gather_scores(scores, groups, lanes):
-    dma = pltpu.SemaphoreType.DMA
-    vmem = pl.BlockSpec(memory_space=pltpu.VMEM)
-    return pl.pallas_call(
-        functools.partial(score_kernel, groups, lanes),
-        out_shape=jax.ShapeDtypeStruct((groups, lanes) + scores.shape, scores.dtype),
-        in_specs=[vmem],
-        out_specs=vmem,
-        scratch_shapes=[
-            dma((lanes - 1,)),
-            dma((lanes - 1,)),
-            dma((groups - 1,)),
-            dma((groups - 1,)),
-        ],
-        compiler_params=pltpu.CompilerParams(
-            collective_id=2, has_side_effects=True, vmem_limit_bytes=8 << 20
-        ),
-        name="gather_scores",
-    )(scores)
+def whole_tables(half_ref, whole_ref, sign):
+    quarter = half_ref.shape[1]
+    for k in range(RADIX):
+        cosine, sine = half_ref[k, :, :quarter], half_ref[k, :, quarter:]
+        upper, lower = (-sine, sine) if sign > 0 else (sine, -sine)
+        whole_ref[k, :quarter, :quarter] = cosine
+        whole_ref[k, :quarter, quarter:] = upper
+        whole_ref[k, quarter:, :quarter] = lower
+        whole_ref[k, quarter:, quarter:] = cosine
 
 
 def plan_kernel(slots, count_ref, cell_ref, band_ref, cells_out, inverse_out, wave_out, route_out):
@@ -523,8 +326,8 @@
 
 
 def focal_kernel(
-    groups, lanes, cell_ref, inverse_ref, route_ref, coef_ref, maps_ref, cot_ref, right_ref, left_ref,
-    turns_out, xr, xi, maps_buf, stage, raw, pool, x_stage, y_stage, z_stage, ct, ct_turned,
+    groups, lanes, cell_ref, inverse_ref, route_ref, coef_ref, maps_ref, cot_ref, right_half, left_half,
+    turns_out, xr, xi, right_ref, left_ref, maps_buf, stage, raw, pool, x_stage, y_stage, z_stage, ct, ct_turned,
     order, spread, yr, yi, *scratch,
 ):
     steps = TURN_STEPS
@@ -572,6 +375,8 @@
 
     fetch(0).start()
     fetch(1).start()
+    whole_tables(right_half, right_ref, -1)
+    whole_tables(left_half, left_ref, 1)
 
     lines = lanes * ROWS_STEP
     wide = map_count * ROWS_STEP
@@ -790,6 +595,8 @@
         in_specs=[smem, smem, smem, vmem, hbm, hbm, vmem, vmem],
         out_specs=(vmem,) * 3,
         scratch_shapes=[
+            pltpu.VMEM((RADIX, half, half), BF16),
+            pltpu.VMEM((RADIX, half, half), BF16),
             pltpu.VMEM((2, map_count, depth, size), BF16),
             pltpu.VMEM((lanes, row_count, size), BF16),
             pltpu.VMEM((2 * slots, row_count, half), BF16),
@@ -829,84 +636,355 @@
     )(cells, inverse, route, coef_table, feature_maps, cotangent, right, left)
 
 
-def column_kernel(chunk, wave_ref, turns_ref, xr, xi, left_ref, out_ref):
-    size = turns_ref.shape[1]
+def gradient_kernel(
+    groups, lanes, cell_ref, wave_ref, coef_ref, turns_ref, xr, xi, half_ref, maps_ref, grad_out, coef_out,
+    left, gathered, away, maps_buf, sums_buf, score, weights, row_part, star_part,
+    m_sem, o_sem, z_send, z_recv, p_send, p_recv, c_send, c_recv, sr_send, sr_recv, ss_send, ss_recv,
+):
+    row = lax.axis_index("row")
+    me = lax.axis_index("star")
+    steps = GATHER_STEPS
+    share = sums_buf.shape[1]
+    map_count, row_count, size = maps_ref.shape
+    depth = row_count // steps
+    parts = depth // ROWS_STEP
     quarter = size // RADIX
+    total = groups * lanes
+    core = me + 1 - 2 * (me % 2)
+    across = me + 2 - 4 * ((me // 2) % 2)
+    along = me + 4 - 8 * ((me // 4) % 2)
+    corner = across + 4 - 8 * ((me // 4) % 2)
+    row_peers = [{"row": (row + d) % lanes} for d in range(1, lanes)]
+    star_peers = [{"star": (me + d) % groups} for d in range(1, groups)]
+    to_core, to_across, to_along = {"star": core}, {"star": across}, {"star": along}
+    greet(row_peers + star_peers)
+    half_lanes = lanes // 2
+
+    def fetch(step, part):
+        rows = pl.ds(pl.multiple_of(step * depth + part * ROWS_STEP, ROWS_STEP), ROWS_STEP)
+        return pltpu.make_async_copy(maps_ref.at[:, rows], maps_buf.at[part], m_sem.at[part])
+
+    for part in range(parts):
+        fetch(0, part).start()
+    whole_tables(half_ref, left, 1)
+
+    def cell_of(group, d):
+        return cell_ref[group * lanes + (row + lanes - d) % lanes]
+
+    at = lax.broadcasted_iota(jnp.int32, (total, coef_ref.shape[0]), 0)
+    to = lax.broadcasted_iota(jnp.int32, (total, coef_ref.shape[0]), 1)
+    wanted = jnp.zeros_like(at)
+    for group in range(groups):
+        for d in range(lanes):
+            wanted = jnp.where(at == group * lanes + d, cell_of(group, d), wanted)
+    hot = jnp.where(to == wanted, 1.0, 0.0).astype(BF16)
+    rows_of = jnp.dot(hot, coef_ref[...], preferred_element_type=F32).astype(BF16)
+    lines = share * ROWS_STEP
+    wide = total * ROWS_STEP
+    at = lax.broadcasted_iota(jnp.int32, (lines, map_count), 0)
+    to = lax.broadcasted_iota(jnp.int32, (lines, map_count), 1)
+    mine = jnp.where(to == me * share + at // ROWS_STEP, 1.0, 0.0).astype(BF16)
+    columns = lax.dot_general(
+        mine, rows_of, (((1,), (1,)), ((), ())), preferred_element_type=F32
+    ).astype(BF16)
+    at = lax.broadcasted_iota(jnp.int32, (total, wide), 0)
+    to = lax.broadcasted_iota(jnp.int32, (total, wide), 1)
+    repeat = jnp.where(to // ROWS_STEP == at, 1.0, 0.0).astype(BF16)
+    repeated = jnp.dot(columns, repeat, preferred_element_type=F32)
+    at = lax.broadcasted_iota(jnp.int32, (lines, wide), 0)
+    to = lax.broadcasted_iota(jnp.int32, (lines, wide), 1)
+    weights[...] = jnp.where(at % ROWS_STEP == to % ROWS_STEP, repeated, 0.0).astype(BF16)
+    score[...] = jnp.zeros_like(score)
+
     blocks = [slice(m * quarter, (m + 1) * quarter) for m in range(RADIX)]
     centre = 0.5 * (size - 1)
-
-    def inverse_columns(step, carry):
-        rows = pl.ds(pl.multiple_of(step * chunk, chunk), chunk)
-        cosine, sine = turn_cos_sin(turns_ref[rows, :].astype(F32))
-        row_pos = (
-            lax.broadcasted_iota(jnp.int32, (chunk, size), 0) + step * chunk
-        ).astype(F32) - centre
-        col_pos = lax.broadcasted_iota(jnp.int32, (chunk, size), 1).astype(F32) - centre
+    tile = lanes * depth
+
+    def rows_at(step):
+        return pl.ds(pl.multiple_of(step * depth, depth), depth)
+
+    def block(group, step, first=0, count=lanes):
+        return gathered.at[group, pl.ds(first, count), rows_at(step)]
+
+    def z_copies(step):
+        return [
+            send(
+                away.at[d - 1, rows_at(step)],
+                gathered.at[me, d, rows_at(step)],
+                z_send.at[step, d - 1],
+                z_recv.at[step, d - 1],
+                row_peers[d - 1],
+            )
+            for d in range(1, lanes)
+        ]
+
+    def plane(step, way, part, peer):
+        return send(part, part, p_send.at[step, way], p_recv.at[step, way], peer)
+
+    def twin(step, way, part):
+        return send(part, part, c_send.at[step, way], c_recv.at[step, way], to_core)
+
+    def sides_own(step):
+        part = block(me, step, 0, 1)
+        return [plane(step, 0, part, to_across), plane(step, 1, part, to_along)]
+
+    def sides_rest(step):
+        part = block(me, step, 1, lanes - 1)
+        return [plane(step, 2, part, to_across), plane(step, 3, part, to_along)]
+
+    def corners(step):
+        return [
+            plane(step, 4, block(across, step, 0, half_lanes), to_along),
+            plane(step, 5, block(along, step, half_lanes, lanes - half_lanes), to_across),
+        ]
+
+    def twins(step, first=0, last=5):
+        parts = [
+            lambda: block(me, step, 0, 1),
+            lambda: block(me, step, 1, lanes - 1),
+            lambda: block(across, step),
+            lambda: block(along, step),
+            lambda: block(corner, step),
+        ]
+        return [twin(step, way, parts[way]()) for way in range(first, last)]
+
+    def columns_step(step):
+        firsts = [(row + d) % lanes * row_count + step * depth for d in range(lanes)]
+        rows = [pl.ds(pl.multiple_of(first, depth), depth) for first in firsts]
+        turns = jnp.concatenate([turns_ref[r, :] for r in rows], 0)
+        cosine, sine = turn_cos_sin(turns.astype(F32))
+        line = lax.broadcasted_iota(jnp.int32, (tile, size), 0)
+        place = (line // depth + row) % lanes * row_count + line % depth + step * depth
+        row_pos = place.astype(F32) - centre
+        col_pos = lax.broadcasted_iota(jnp.int32, (tile, size), 1).astype(F32) - centre
         inside = row_pos * row_pos + col_pos * col_pos <= 0.25 * size * size
         real = jnp.where(inside, cosine, 0.0)
         imag = jnp.where(inside, sine, 0.0)
         part_real, part_imag = [], []
         for k in range(RADIX):
-            both = jnp.concatenate([xr[rows, blocks[k]], xi[rows, blocks[k]]], 1)
-            made = jnp.dot(both, left_ref[k], preferred_element_type=F32)
+            both = jnp.concatenate(
+                [
+                    jnp.concatenate([xr[r, blocks[k]] for r in rows], 0),
+                    jnp.concatenate([xi[r, blocks[k]] for r in rows], 0),
+                ],
+                1,
+            )
+            made = jnp.dot(both, left[k], preferred_element_type=F32)
             part_real.append(made[:, :quarter])
             part_imag.append(made[:, quarter:])
         grad_real, grad_imag = butterfly(part_real, part_imag, 1)
-        wave = wave_ref[0]
+        wave = wave_ref[me * lanes + row]
         for m in range(RADIX):
             grad = real[:, blocks[m]] * grad_imag[m] - imag[:, blocks[m]] * grad_real[m]
-            out_ref[rows, blocks[m]] = (wave * grad).astype(BF16)
+            grad = (wave * grad).astype(BF16)
+            gathered[me, 0, rows_at(step), blocks[m]] = grad[:depth]
+            for d in range(1, lanes):
+                away[d - 1, rows_at(step), blocks[m]] = grad[d * depth : (d + 1) * depth]
+
+    def score_step(step):
+        for part in range(parts):
+            fetch(step, part).wait()
+            rows = pl.ds(pl.multiple_of(step * depth + part * ROWS_STEP, ROWS_STEP), ROWS_STEP)
+            grads = gathered[me, :, rows].reshape(lanes * ROWS_STEP, size)
+            maps = maps_buf[part].reshape(map_count * ROWS_STEP, size)
+            score[...] += lax.dot_general(
+                maps, grads, (((1,), (1,)), ((), ())), preferred_element_type=F32
+            )
+
+            @pl.when(step + 1 < steps)
+            def _():
+                fetch(step + 1, part).start()
+
+    def sums_out(step):
+        return pltpu.make_async_copy(
+            sums_buf.at[step % 2], grad_out.at[:, rows_at(step)], o_sem.at[step % 2]
+        )
+
+    def sums_step(step):
+        @pl.when(step >= 2)
+        def _():
+            sums_out(step - 2).wait()
+
+        for part in range(parts):
+            rows = pl.ds(pl.multiple_of(step * depth + part * ROWS_STEP, ROWS_STEP), ROWS_STEP)
+            grads = gathered[:, :, rows].reshape(wide, size)
+            made = jnp.dot(weights[...], grads, preferred_element_type=F32)
+            sums_buf[step % 2, :, pl.ds(part * ROWS_STEP, ROWS_STEP)] = made.reshape(
+                share, ROWS_STEP, size
+            )
+        sums_out(step).start()
+
+    def row_copies():
+        return [
+            send(row_part.at[row], row_part.at[row], sr_send.at[d], sr_recv.at[d], row_peers[d])
+            for d in range(lanes - 1)
+        ]
+
+    def star_copies():
+        return [
+            send(star_part.at[me], star_part.at[me], ss_send.at[d], ss_recv.at[d], star_peers[d])
+            for d in range(groups - 1)
+        ]
+
+    def scores_rows():
+        lined = score[...]
+        at = lax.broadcasted_iota(jnp.int32, lined.shape, 0)
+        to = lax.broadcasted_iota(jnp.int32, lined.shape, 1)
+        kept = jnp.where(at % ROWS_STEP == to % ROWS_STEP, lined, 0.0)
+        kept = jnp.sum(kept.reshape(map_count, ROWS_STEP, lined.shape[1]), axis=1)
+        to = lax.broadcasted_iota(jnp.int32, kept.shape, 1)
+        cell = lax.broadcasted_iota(jnp.int32, row_part.shape[1:], 1)
+        part = jnp.zeros(row_part.shape[1:], F32)
+        for d in range(lanes):
+            value = jnp.sum(jnp.where(to // ROWS_STEP == d, kept, 0.0), axis=1, keepdims=True)
+            part += jnp.where(cell == cell_of(me, d), value, 0.0)
+        row_part[row] = part
+        for copy in row_copies():
+            copy.start()
+
+    def scores_stars():
+        for copy in row_copies():
+            copy.wait()
+        star_part[me] = jnp.sum(row_part[...], axis=0)
+        for copy in star_copies():
+            copy.start()
+
+    def scores_end():
+        for copy in star_copies():
+            copy.wait()
+        summed = jnp.sum(star_part[...], axis=0) * (1.0 / (8 * size))
+        coef_out[...] = summed.T[: coef_out.shape[0]]
+
+    def between(tick, lag, body):
+        @pl.when(jnp.logical_and(tick >= lag, tick < steps + lag))
+        def _():
+            body(tick - lag)
+
+    def compute(step):
+        columns_step(step)
+        for copy in z_copies(step) + sides_own(step) + twins(step, 0, 1):
+            copy.start()
+
+    def own_arrived(step):
+        for copy in z_copies(step):
+            copy.wait_recv()
+        for copy in sides_rest(step) + twins(step, 1, 2):
+            copy.start()
+
+    def sides_arrived(step):
+        for copy in sides_own(step) + sides_rest(step):
+            copy.wait_recv()
+        for copy in corners(step) + twins(step, 2, 4):
+            copy.start()
+
+    def corners_arrived(step):
+        for copy in corners(step):
+            copy.wait_recv()
+        for copy in twins(step, 4):
+            copy.start()
+
+    def all_arrived(step):
+        for copy in twins(step):
+            copy.wait_recv()
+        sums_step(step)
+
+    def tick_body(tick, carry):
+        between(tick, 0, compute)
+        between(tick, 1, own_arrived)
+        between(tick, 2, sides_arrived)
+        between(tick, 3, corners_arrived)
+        between(tick, 1, score_step)
+
+        @pl.when(tick == steps)
+        def _():
+            scores_rows()
+
+        @pl.when(tick == steps + 1)
+        def _():
+            scores_stars()
+
+        @pl.when(tick == steps + 2)
+        def _():
+            scores_end()
+
+        between(tick, 4, all_arrived)
         return carry
 
-    lax.fori_loop(0, size // chunk, inverse_columns, 0)
-
-
-def column_gradient(wave, turns, spec_real, spec_imag, left):
+    lax.fori_loop(0, steps + 4, tick_body, 0)
+
+    def drain(step, carry):
+        for copy in (
+            z_copies(step) + sides_own(step) + sides_rest(step) + corners(step) + twins(step)
+        ):
+            copy.wait_send()
+        return carry
+
+    lax.fori_loop(0, steps, drain, 0)
+    for step in range(steps - 2, steps):
+        sums_out(step).wait()
+
+
+def gradient_sums(cells, wave, coef_table, turns, spec_real, spec_imag, halves, feature_maps, groups, lanes):
+    map_count, row_count, size = feature_maps.shape
+    cell_count = coef_table.shape[0]
+    share = map_count // groups
+    depth = row_count // GATHER_STEPS
+    dma = pltpu.SemaphoreType.DMA
+    smem = pl.BlockSpec(memory_space=pltpu.SMEM)
     vmem = pl.BlockSpec(memory_space=pltpu.VMEM)
+    hbm = pl.BlockSpec(memory_space=pl.ANY)
+    half = size // 2
+    padded = -(-cell_count // 128) * 128
     return pl.pallas_call(
-        functools.partial(column_kernel, 128),
-        out_shape=jax.ShapeDtypeStruct(turns.shape, BF16),
-        in_specs=[pl.BlockSpec(memory_space=pltpu.SMEM), vmem, vmem, vmem, vmem],
-        out_specs=vmem,
-        compiler_params=pltpu.CompilerParams(vmem_limit_bytes=56 << 20),
-        name="column_gradient",
-    )(wave, turns, spec_real, spec_imag, left)
+        functools.partial(gradient_kernel, groups, lanes),
+        out_shape=(
+            jax.ShapeDtypeStruct((share, row_count, size), F32),
+            jax.ShapeDtypeStruct((cell_count, map_count), F32),
+        ),
+        in_specs=[smem, smem, vmem, vmem, vmem, vmem, vmem, hbm],
+        out_specs=(hbm, vmem),
+        scratch_shapes=[
+            pltpu.VMEM((RADIX, half, half), BF16),
+            pltpu.VMEM((groups, lanes, row_count, size), BF16),
+            pltpu.VMEM((lanes - 1, row_count, size), BF16),
+            pltpu.VMEM((depth // ROWS_STEP, map_count, ROWS_STEP, size), BF16),
+            pltpu.VMEM((2, share, depth, size), F32),
+            pltpu.VMEM((map_count * ROWS_STEP, lanes * ROWS_STEP), F32),
+            pltpu.VMEM((share * ROWS_STEP, groups * lanes * ROWS_STEP), BF16),
+            pltpu.VMEM((lanes, map_count, padded), F32),
+            pltpu.VMEM((groups, map_count, padded), F32),
+            dma((depth // ROWS_STEP,)),
+            dma((2,)),
+            dma((GATHER_STEPS, lanes - 1)),
+            dma((GATHER_STEPS, lanes - 1)),
+            dma((GATHER_STEPS, 6)),
+            dma((GATHER_STEPS, 6)),
+            dma((GATHER_STEPS, 5)),
+            dma((GATHER_STEPS, 5)),
+            dma((lanes - 1,)),
+            dma((lanes - 1,)),
+            dma((groups - 1,)),
+            dma((groups - 1,)),
+        ],
+        compiler_params=pltpu.CompilerParams(
+            collective_id=1, has_side_effects=True, vmem_limit_bytes=60 << 20
+        ),
+        name="gradient_sums",
+    )(cells, wave, coef_table, turns, spec_real, spec_imag, halves, feature_maps)
 
 
 def star_devices(feature_maps, coef_table, star_counts, star_cells, star_bands, psf_cotangent):
     groups = lax.axis_size("star")
     lanes = lax.axis_size("row")
-    my_group = lax.axis_index("star")
-    my_lane = lax.axis_index("row")
-    map_count, row_count, size = feature_maps.shape
-    cell_count = coef_table.shape[0]
-    share = map_count // groups
-    total = groups * lanes
-    cell_ids, inverse, wave, route = plan(star_counts, star_cells, star_bands)
-    cell_hot = cell_ids[:, None] == jnp.arange(cell_count, dtype=jnp.int32)[None, :]
-    coef_rows = jnp.dot(
-        cell_hot.astype(BF16), coef_table, preferred_element_type=F32
-    ).astype(BF16)
-    right, left = quarter_tables(size)
+    size = feature_maps.shape[2]
+    cells, inverse, wave, route = plan(star_counts, star_cells, star_bands)
+    right, left = half_tables(size)
     turns, spec_real, spec_imag = focal_fields(
-        cell_ids, inverse, route, coef_table, feature_maps, psf_cotangent, right, left, groups, lanes
-    )
-    my_wave = lax.dynamic_slice_in_dim(wave, my_group * lanes + my_lane, 1, 0)
-    path_grad = column_gradient(my_wave, turns, spec_real, spec_imag, left)
-    path_grads = gather_grads(path_grad.reshape(lanes, row_count, size), groups)
-    path_grads = path_grads.reshape(total, row_count, size)
-    my_coefs = lax.dynamic_slice_in_dim(coef_rows.T, my_group * share, share, 0)
-    map_grad, scores = map_sums(my_group, my_coefs, path_grads, feature_maps, share)
-    scores = jnp.pad(scores, ((0, 0), (0, -total % 128)))
-    scores = jnp.sum(gather_scores(scores, groups, lanes), axis=1)
-    scores = scores.reshape(map_count, -1)[:, :total]
-    coef_grad = lax.dot_general(
-        cell_hot.astype(F32),
-        scores * (1.0 / (8 * size)),
-        (((0,), (1,)), ((), ())),
-        precision=lax.Precision.HIGHEST,
-    )
-    return map_grad, coef_grad
+        cells, inverse, route, coef_table, feature_maps, psf_cotangent, right, left, groups, lanes
+    )
+    return gradient_sums(
+        cells, wave, coef_table, turns, spec_real, spec_imag, left, feature_maps, groups, lanes
+    )
 
 
 def solution(mesh):

time: 254 us -> 212 us (0.83); the launches traced: 249 us -> 211 us
  Pallas kernels: 241 us -> 201 us
  local copies, waits for them, and re-layouts: 5.52 us -> 9.07 us
    pallas_call x4 -> x1, Pallas kernels: 131 us -> 91.7 us  [gradient_sums(): pl.pallas_call(functools.partial(gradient_kernel, groups, lanes), out_sha...]
    unnamed x4, local copies, waits for them, and re-layouts: 0.01 us -> 9.07 us
where the time goes in v2:
time: 212 us; the launch traced here: 211 us
  Pallas kernels  201 us (95%)
  local copies, waits for them, and re-layouts  9.07 us (4%)
    pallas_call x1, Pallas kernels, focal_fields(): pl.pallas_call(functools.partial(focal_kernel, groups, lanes), out_shape=...  107 us
    pallas_call x1, Pallas kernels, gradient_sums(): pl.pallas_call(functools.partial(gradient_kernel, groups, lanes), out_sha...  91.7 us
    unnamed x4, local copies, waits for them, and re-layouts  9.07 us

profile of v2, /device:TPU:27, one launch (start us, length us, event | category | flops | bytes accessed | tf_op | source)
XLA Modules:
  0.0 210.9 jit_solution(3978912993970023468)
XLA Ops:
  0.6 2.9 %plan.1 = (s32[32]{0:T(128)}, f32[32]{0:T(128)}, f32[32]{0:T(128)}, s32[100]{0:T(128)}) custom-call(s32[8]{0:T(128)} %count_ref.1, s32[8,12]{1,0:T(8,128)} %cell_ref.1, s32[8,12]{1,0:T(8,128)} %band_ref.1), custom_call_target="tpu_custom_call" | custom-call | tf_op jit(solution)/shard_map/plan/pallas_call | solution.py:307
  3.5 106.6 %focal_fields.1 = (bf16[1024,1024]{1,0:T(8,128)(2,1)}, bf16[1024,1024]{1,0:T(8,128)(2,1)}, bf16[1024,1024]{1,0:T(8,128)(2,1)}) custom-call(s32[32]{0:T(128)} %get-tuple-element.9.cell_ref, f32[32]{0:T(128)} %get-tuple-element.11.inverse_ref, s32[100]{0:T(128)} %get-tuple-element.12.route_ref, bf16[64,64]{1,0:T(8,128)(2,1)} %coef_ref.3, ...), custom_call_target="tpu_custom_call" | custom-call | tf_op jit(solution)/shard_map/focal_fields/pallas_call | solution.py:592
  110.1 91.7 %gradient_sums.1 = (f32[8,256,1024]{2,1,0:T(8,128)}, f32[64,64]{1,0:T(8,128)}) custom-call(s32[32]{0:T(128)} %get-tuple-element.9.cell_ref, f32[32]{0:T(128)} %get-tuple-element.10.wave_ref, bf16[64,64]{1,0:T(8,128)(2,1)} %coef_ref.3, bf16[1024,1024]{1,0:T(8,128)(2,1)} %get-tuple-element.13.turns_ref, bf16[1024,1024]{1,0:T(8,128)(2,1)} %get-tuple-element.14.xr, ...), custom_call_target="tpu_custom_call" | custom-call | tf_op jit(solution)/shard_map/gradient_sums/pallas_call | solution.py:938
  201.8 0.0 copy-start
  201.8 8.4 %copy.12 = f32[8,256,1024]{2,1,0:T(8,128)} copy(f32[8,256,1024]{2,1,0:T(8,128)} %get-tuple-element.18) | data formatting | bytes 16777216
  210.3 0.0 copy-done
  210.3 0.6 copy.13
Async XLA Ops:
  201.8 8.5 %copy-start = (f32[64,64]{1,0:T(8,128)S(1)}, f32[64,64]{1,0:T(8,128)}, u32[]{:S(2)}) copy-start(f32[64,64]{1,0:T(8,128)} %get-tuple-element.19) | copy-start | bytes 49156

commit v3 on v2

--- a/solution.py
+++ b/solution.py
@@ -17,9 +17,14 @@
 EARLY_STEPS = 2
 ROUTE_CHUNKS = 8
 GATHER_STEPS = 8
+Z_AHEAD = 2
+SIDES_LAG = 2
+CORNERS_LAG = 2
 OVER_X = 11
 OVER_Y = 6
 STARS_CHIP = 8
+K1_LIMIT = 47
+K2_LIMIT = 34
 F32 = jnp.float32
 BF16 = jnp.bfloat16
 
@@ -163,12 +168,8 @@
     freq = RADIX * np.arange(quarter)[None, None, :] + np.arange(RADIX)[:, None, None]
     angle = 2.0 * np.pi / size * ((place * freq) % size)
     cosine, sine = np.cos(angle), -np.sin(angle)
-    right = np.concatenate([cosine, sine], 2).astype(np.float32)
-    left = np.concatenate([np.swapaxes(cosine, 1, 2), np.swapaxes(sine, 1, 2)], 2)
-    return (
-        jnp.asarray(right.astype(jnp.bfloat16)),
-        jnp.asarray(left.astype(np.float32).astype(jnp.bfloat16)),
-    )
+    table = np.concatenate([cosine, sine], 2).astype(np.float32)
+    return jnp.asarray(table.astype(jnp.bfloat16))
 
 
 def turn_cos_sin(turns):
@@ -201,7 +202,10 @@
     barrier = pltpu.get_barrier_semaphore()
     for peer in peers:
         pl.semaphore_signal(barrier, inc=1, device_id=peer, device_id_type=pl.DeviceIdType.MESH)
-    pl.semaphore_wait(barrier, len(peers))
+
+
+def greeted(peers):
+    pl.semaphore_wait(pltpu.get_barrier_semaphore(), len(peers))
 
 
 def send(source, target, send_sem, recv_sem, peer):
@@ -215,21 +219,39 @@
     )
 
 
-def whole_tables(half_ref, whole_ref, sign):
+def right_tables(half_ref, whole_ref):
     quarter = half_ref.shape[1]
     for k in range(RADIX):
         cosine, sine = half_ref[k, :, :quarter], half_ref[k, :, quarter:]
-        upper, lower = (-sine, sine) if sign > 0 else (sine, -sine)
         whole_ref[k, :quarter, :quarter] = cosine
-        whole_ref[k, :quarter, quarter:] = upper
-        whole_ref[k, quarter:, :quarter] = lower
+        whole_ref[k, :quarter, quarter:] = sine
+        whole_ref[k, quarter:, :quarter] = -sine
         whole_ref[k, quarter:, quarter:] = cosine
 
 
-def plan_kernel(slots, count_ref, cell_ref, band_ref, cells_out, inverse_out, wave_out, route_out):
+def left_tables(half_ref, whole_ref):
+    quarter = half_ref.shape[1]
+    at = lax.broadcasted_iota(jnp.int32, (quarter, quarter), 0)
+    to = lax.broadcasted_iota(jnp.int32, (quarter, quarter), 1)
+    same = jnp.where(at == to, 1.0, 0.0).astype(BF16)
+
+    def turned(table):
+        made = lax.dot_general(same, table, (((1,), (1,)), ((), ())), preferred_element_type=F32)
+        return made.astype(BF16)
+
+    def fill(k, carry):
+        cosine, sine = turned(half_ref[k, :, :quarter]), turned(half_ref[k, :, quarter:])
+        whole_ref[k, :quarter, :quarter] = cosine
+        whole_ref[k, :quarter, quarter:] = -sine
+        whole_ref[k, quarter:, :quarter] = sine
+        whole_ref[k, quarter:, quarter:] = cosine
+        return carry
+
+    lax.fori_loop(0, RADIX, fill, 0)
+
+
+def star_plan(slots, count_ref, cells_ref, bands_ref):
     chips = count_ref.shape[0] // 2
-    over_x, over_y = OVER_X, OVER_Y
-    share = STARS_CHIP
     first = [count_ref[2 * c] for c in range(chips)]
     held = [first[c] + count_ref[2 * c + 1] for c in range(chips)]
     level = []
@@ -238,9 +260,9 @@
         if y == 0:
             level += [both // 2, both - both // 2]
         else:
-            level += [2 * share - level[0], 2 * share - level[1]]
+            level += [2 * STARS_CHIP - level[0], 2 * STARS_CHIP - level[1]]
     keep_x = [jnp.minimum(held[c], level[c]) for c in range(chips)]
-    keep_y = [jnp.minimum(level[c], share) for c in range(chips)]
+    keep_y = [jnp.minimum(level[c], STARS_CHIP) for c in range(chips)]
 
     def choose(values, index):
         out = values[0]
@@ -248,74 +270,66 @@
             out = jnp.where(index == c, values[c], out)
         return out
 
-    def slot_of(chip, place):
-        place = jnp.minimum(place, choose(held, chip) - 1)
-        start = choose(first, chip)
-        return jnp.where(place < start, place, slots + place - start)
-
-    def after_x(chip, place):
-        place = jnp.minimum(place, choose(level, chip) - 1)
-        kept = choose(keep_x, chip)
-        return jnp.where(place < kept, slot_of(chip, place), 2 * slots + place - kept)
-
-    def star_x(chip, place):
-        kept = choose(keep_x, chip)
-        other = chip + 1 - 2 * (chip % 2)
-        own = chip * 2 * slots + slot_of(chip, place)
-        far = other * 2 * slots + slot_of(other, choose(keep_x, other) + place - kept)
-        return jnp.where(place < kept, own, far)
-
-    per_chip = over_x + over_y + share
-
-    def fill(chip, carry):
-        base = chip * per_chip
+    def routes(chip):
+        start, count, reached = choose(first, chip), choose(held, chip), choose(level, chip)
         kept_x, kept_y = choose(keep_x, chip), choose(keep_y, chip)
-        for i in range(over_x):
-            route_out[base + i] = slot_of(chip, kept_x + i)
-        for i in range(over_y):
-            route_out[base + over_x + i] = after_x(chip, kept_y + i)
-        other = chip + 2 - 4 * (chip // 2)
-        for i in range(share):
-            from_y = 2 * slots + over_x + i - kept_y
-            route_out[base + over_x + over_y + i] = jnp.where(
-                i < kept_y, after_x(chip, i), from_y
+
+        def slot_of(place):
+            place = jnp.minimum(place, count - 1)
+            return jnp.where(place < start, place, slots + place - start)
+
+        def after_x(place):
+            place = jnp.minimum(place, reached - 1)
+            return jnp.where(place < kept_x, slot_of(place), 2 * slots + place - kept_x)
+
+        def after_y(place):
+            return jnp.where(
+                place < kept_y, after_x(place), 2 * slots + OVER_X + place - kept_y
             )
-            star = jnp.where(
-                i < kept_y, star_x(chip, i), star_x(other, choose(keep_y, other) + i - kept_y)
-            )
-            group = star // slots
-            band = band_ref[group, star - group * slots]
-            at = chip * share + i
-            cells_out[at] = cell_ref[group, star - group * slots]
-            inverse, wave = jnp.float32(0), jnp.float32(0)
-            for b in range(BANDS):
-                length = 0.55 + 0.35 * b / (BANDS - 1)
-                inverse = jnp.where(band == b, np.float32(1.0 / length), inverse)
-                wave = jnp.where(band == b, np.float32(2.0 * np.pi / length), wave)
-            inverse_out[at] = inverse
-            wave_out[at] = wave
-        return carry
-
-    lax.fori_loop(0, chips, fill, 0)
-
-
-def plan(star_counts, star_cells, star_bands):
-    smem = pl.BlockSpec(memory_space=pltpu.SMEM)
-    groups, slots = star_cells.shape
-    chips = groups // 2
-    total = chips * STARS_CHIP
-    return pl.pallas_call(
-        functools.partial(plan_kernel, slots),
-        out_shape=(
-            jax.ShapeDtypeStruct((total,), jnp.int32),
-            jax.ShapeDtypeStruct((total,), F32),
-            jax.ShapeDtypeStruct((total,), F32),
-            jax.ShapeDtypeStruct((chips * (OVER_X + OVER_Y + STARS_CHIP),), jnp.int32),
-        ),
-        in_specs=[smem] * 3,
-        out_specs=(smem,) * 4,
-        name="plan",
-    )(star_counts, star_cells, star_bands)
+
+        return (
+            [jnp.clip(slot_of(kept_x + i), 0, 2 * slots - 1) for i in range(OVER_X)]
+            + [after_x(kept_y + i) for i in range(OVER_Y)]
+            + [after_y(i) for i in range(STARS_CHIP)]
+        )
+
+    def star_at(chip, place):
+        over_y = chip + 2 - 4 * (chip // 2)
+        kept_y = choose(keep_y, chip)
+        here = jnp.where(place < kept_y, chip, over_y)
+        place = jnp.where(place < kept_y, place, choose(keep_y, over_y) + place - kept_y)
+        over_x = here + 1 - 2 * (here % 2)
+        kept_x = choose(keep_x, here)
+        origin = jnp.where(place < kept_x, here, over_x)
+        place = jnp.where(place < kept_x, place, choose(keep_x, over_x) + place - kept_x)
+        inner = place < choose(first, origin)
+        group = 2 * origin + jnp.where(inner, 0, 1)
+        slot = jnp.where(inner, place, place - choose(first, origin))
+        return jnp.clip(group, 0, 2 * chips - 1), jnp.clip(slot, 0, slots - 1)
+
+    def cell_at(chip, place):
+        group, slot = star_at(chip, place)
+        return cells_ref[group, slot]
+
+    def wave_at(chip, place, scale):
+        group, slot = star_at(chip, place)
+        band = bands_ref[group, slot]
+        value = jnp.float32(0)
+        for b in range(BANDS):
+            length = 0.55 + 0.35 * b / (BANDS - 1)
+            value = jnp.where(band == b, np.float32(scale / length), value)
+        return value
+
+    return routes, cell_at, wave_at
+
+
+def aperture_widths(size, row_count, depth):
+    widths = []
+    for step in range(row_count // depth):
+        lowest = abs(step * depth + depth - 1 - 0.5 * (size - 1))
+        reach = 2 * (np.sqrt(0.25 * size * size - lowest * lowest) + 1)
+        widths.append(min(size, int(-(-reach // 256) * 256)))
+    return widths
 
 
 def group_rows(step, depth, row_count, lanes):
@@ -326,11 +340,20 @@
 
 
 def focal_kernel(
-    groups, lanes, cell_ref, inverse_ref, route_ref, coef_ref, maps_ref, cot_ref, right_half, left_half,
-    turns_out, xr, xi, right_ref, left_ref, maps_buf, stage, raw, pool, x_stage, y_stage, z_stage, ct, ct_turned,
-    order, spread, yr, yi, *scratch,
+    groups, lanes, count_hbm, cells_hbm, bands_hbm, coef_hbm, maps_ref, cot_ref, half_ref,
+    turns_out, xr, xi, left_ref, right_ref, maps_buf, stage, raw, pool, x_stage, y_stage, ct, ct_turned,
+    spread, yr, yi, route_ref, count_ref, cells_ref, bands_ref, coef_ref,
+    small_sem, *scratch,
 ):
     steps = TURN_STEPS
+    small = [
+        pltpu.make_async_copy(count_hbm, count_ref, small_sem.at[0]),
+        pltpu.make_async_copy(cells_hbm, cells_ref, small_sem.at[1]),
+        pltpu.make_async_copy(bands_hbm, bands_ref, small_sem.at[2]),
+        pltpu.make_async_copy(coef_hbm, coef_ref, small_sem.at[3]),
+    ]
+    for copy in small:
+        copy.start()
     chunks = pool.shape[0]
     x_got, y_got = scratch[:chunks], scratch[chunks : 2 * chunks]
     (
@@ -344,14 +367,15 @@
     twin = me + 1 - 2 * core
     over_x = me + 2 - 4 * (chip % 2)
     over_y = me + 4 - 8 * (me // 4)
-    map_count, depth, size = maps_buf.shape[1:]
-    row_count = depth * steps
+    map_count, row_count, size = maps_ref.shape
+    depth = row_count // steps
     half = size // 2
     quarter = size // RADIX
     slots = raw.shape[0] // 2
     places = [(d, e) for e in range(2) for d in range(lanes)][1:]
     peers = [{"row": (row + d) % lanes, "star": twin if e else me} for d, e in places]
-    greet(peers + [{"star": over_x}, {"star": over_y}])
+    peers_all = peers + [{"star": over_x}, {"star": over_y}]
+    greet(peers_all)
 
     slot_range = pl.ds(core * slots, slots)
     other = 1 - core
@@ -366,24 +390,26 @@
         {"star": twin},
     )
     raw_own.start()
-    raw_twin.start()
-
-    def fetch(step):
-        slot = step % 2
-        rows = pl.ds(pl.multiple_of(step * depth, depth), depth)
-        return pltpu.make_async_copy(maps_ref.at[:, rows], maps_buf.at[slot], m_sem.at[slot])
-
-    fetch(0).start()
-    fetch(1).start()
-    whole_tables(right_half, right_ref, -1)
-    whole_tables(left_half, left_ref, 1)
+
+    def fetch(step, part):
+        rows = pl.ds(pl.multiple_of(step * depth + part * ROWS_STEP, ROWS_STEP), ROWS_STEP)
+        return pltpu.make_async_copy(maps_ref.at[:, rows], maps_buf.at[part], m_sem.at[part])
+
+    for part in range(depth // ROWS_STEP):
+        fetch(0, part).start()
+    for copy in small:
+        copy.wait()
+    routes, cell_at, wave_at = star_plan(slots, count_ref, cells_ref, bands_ref)
+    places_here = [core * lanes + s for s in range(lanes)]
+    cell_here = [cell_at(chip, place) for place in places_here]
+    turn_here = [wave_at(chip, place, 1.0) for place in places_here]
 
     lines = lanes * ROWS_STEP
     wide = map_count * ROWS_STEP
     cells = lax.broadcasted_iota(jnp.int32, (ROWS_STEP, coef_ref.shape[0]), 1)
     hot = jnp.concatenate(
         [
-            jnp.where(cells == cell_ref[me * lanes + s], 1.0, 0.0).astype(BF16)
+            jnp.where(cells == cell_here[s], 1.0, 0.0).astype(BF16)
             for s in range(lanes)
         ],
         0,
@@ -397,80 +423,117 @@
     to = lax.broadcasted_iota(jnp.int32, (lines, wide), 1)
     spread[...] = jnp.where(at % ROWS_STEP == to % ROWS_STEP, repeated, 0.0).astype(BF16)
 
-    def turn_copies(step):
+    widths = aperture_widths(size, row_count, depth)
+
+    def turn_local(step):
         rows = pl.ds(pl.multiple_of(step * depth, depth), depth)
         place = pl.ds(pl.multiple_of(row * row_count + step * depth, depth), depth)
-        return [
-            pltpu.make_async_copy(stage.at[row, rows], turns_out.at[place], t_local.at[step])
-        ] + [
-            send(
-                stage.at[(row + d) % lanes, rows],
-                turns_out.at[place],
-                t_send.at[step, d - 1],
-                t_recv.at[step, d - 1],
-                {"row": (row + d) % lanes},
+        return pltpu.make_async_copy(stage.at[row, rows], turns_out.at[place], t_local.at[step])
+
+    def turn_copy(step, d, source, width):
+        rows = pl.ds(pl.multiple_of(step * depth, depth), depth)
+        place = pl.ds(pl.multiple_of(source * row_count + step * depth, depth), depth)
+        cols = pl.ds((size - width) // 2, width)
+        return send(
+            stage.at[(row + d) % lanes, rows, cols],
+            turns_out.at[place, cols],
+            t_send.at[step],
+            t_recv.at[step, d - 1],
+            {"row": (row + d) % lanes},
+        )
+
+    def each_width(step, source, body):
+        outer = jnp.where(source == 0, step, jnp.where(source == lanes - 1, steps - 1 - step, steps))
+        first = 0
+        for width in sorted(set(widths) | {size}):
+            last = first + widths.count(width) if width < size else steps + 1
+
+            @pl.when(jnp.logical_and(outer >= first, outer < last))
+            def _():
+                body(width)
+
+            first = last
+
+    def turns_start(step):
+        turn_local(step).start()
+
+        def start(width):
+            for d in range(1, lanes):
+                turn_copy(step, d, row, width).start()
+
+        each_width(step, row, start)
+
+    def turns_wait(step):
+        turn_local(step).wait()
+        rows = pl.ds(pl.multiple_of(step * depth, depth), depth)
+
+        def sent(width):
+            part = stage.at[pl.ds(0, lanes - 1), rows, pl.ds((size - width) // 2, width)]
+            send(part, part, t_send.at[step], t_recv.at[step, 0], peers[0]).wait_send()
+
+        each_width(step, row, sent)
+        for d in range(1, lanes):
+            source = (row + lanes - d) % lanes
+            each_width(
+                step, source, lambda width: turn_copy(step, d, source, width).wait_recv()
             )
-            for d in range(1, lanes)
-        ]
-
-    def phase_step(step, carry):
-        slot = step % 2
-        fetch(step).wait()
+
+    def phase_turns(step, carry):
         for part in range(depth // ROWS_STEP):
-            lined = pl.ds(part * ROWS_STEP, ROWS_STEP)
-            maps = maps_buf[slot, :, lined].reshape(wide, size)
+            fetch(step, part).wait()
+            maps = maps_buf[part].reshape(wide, size)
             path = jnp.dot(spread[...], maps, preferred_element_type=F32)
             rows = pl.ds(pl.multiple_of(step * depth + part * ROWS_STEP, ROWS_STEP), ROWS_STEP)
             for s in range(lanes):
-                turned = path[s * ROWS_STEP : (s + 1) * ROWS_STEP] * inverse_ref[me * lanes + s]
+                turned = path[s * ROWS_STEP : (s + 1) * ROWS_STEP] * turn_here[s]
                 stage[s, rows] = (turned - jnp.floor(turned + 0.5)).astype(BF16)
-        for copy in turn_copies(step):
-            copy.start()
-
-        @pl.when(step + 2 < steps)
-        def _():
-            fetch(step + 2).start()
+
+            @pl.when(step + 1 < steps)
+            def _():
+                fetch(step + 1, part).start()
 
         return carry
 
-    lax.fori_loop(0, EARLY_STEPS, phase_step, 0)
+    def phase_step(step, carry):
+        phase_turns(step, carry)
+        turns_start(step)
+        return carry
 
     def x_copy(c):
-        return send(x_stage.at[c], x_got[c], x_send.at[c], x_recv.at[c], {"star": over_x})
+        return send(x_stage.at[c], x_got[c], x_send, x_recv.at[c], {"star": over_x})
 
     def y_copy(c):
-        return send(y_stage.at[c], y_got[c], y_send.at[c], y_recv.at[c], {"star": over_y})
+        return send(y_stage.at[c], y_got[c], y_send, y_recv.at[c], {"star": over_y})
 
     tall = quarter // lanes
     piece = tall * RADIX // chunks
     parts = chunks // RADIX
-    per_chip = OVER_X + OVER_Y + STARS_CHIP
-    base = chip * per_chip
-
-    def z_copies(c):
+
+    def star_piece(c, star):
+        lined = pl.ds(pl.multiple_of(c * piece, piece), piece)
+        return raw.at[2 * RADIX + star, lined]
+
+    def z_target(c):
         kind, part = c // parts, c % parts
-        target = ct.at[
+        return ct.at[
             kind,
             pl.ds(pl.multiple_of(row * tall + part * piece, piece), piece),
             pl.ds(pl.multiple_of(core * half, half), half),
         ]
-        own = z_stage.at[c, core * lanes + row]
-        return [pltpu.make_async_copy(own, target, z_local.at[c])] + [
-            send(
-                z_stage.at[c, (core + e) % 2 * lanes + (row + d) % lanes],
-                target,
-                z_send.at[c, n],
-                z_recv.at[c, n],
-                peers[n],
-            )
-            for n, (d, e) in enumerate(places)
-        ]
-
-    raw_own.wait()
-    raw_twin.wait()
-    at = lax.broadcasted_iota(jnp.int32, (row_count, row_count), 0)
-    to = lax.broadcasted_iota(jnp.int32, (row_count, row_count), 1)
-    sort = jnp.where(at % tall * RADIX + at // tall == to, 1.0, 0.0).astype(BF16)
+
+    def z_local_copy(c):
+        return pltpu.make_async_copy(star_piece(c, core * lanes + row), z_target(c), z_local.at[c])
+
+    def z_start(c):
+        z_local_copy(c).start()
+        for d, e in places:
+            star = (core + e) % 2 * lanes + (row + d) % lanes
+            peer = {"row": (row + d) % lanes, "star": twin if e else me}
+            send(star_piece(c, star), z_target(c), z_send, z_recv.at[c], peer).start()
+
+    def z_arrival(c):
+        sized = raw.at[pl.ds(0, len(places)), pl.ds(0, piece)]
+        return send(sized, sized, z_send, z_recv.at[c], peers[0])
 
     def sort_slot(slot, carry):
         sorted_rows = jnp.dot(sort, raw[slot], preferred_element_type=F32).astype(BF16)
@@ -478,38 +541,55 @@
             pool[c, slot] = sorted_rows[c * piece : (c + 1) * piece]
         return carry
 
-    lax.fori_loop(0, 2 * slots, sort_slot, 0)
+    phase_turns(0, 0)
+    for i, entry in enumerate(routes(chip)):
+        route_ref[i] = entry
+    at = lax.broadcasted_iota(jnp.int32, (row_count, row_count), 0)
+    to = lax.broadcasted_iota(jnp.int32, (row_count, row_count), 1)
+    sort = jnp.where(at % tall * RADIX + at // tall == to, 1.0, 0.0).astype(BF16)
+    greeted(peers_all)
+    raw_twin.start()
+    turns_start(0)
+    raw_own.wait()
+    lax.fori_loop(core * slots, core * slots + slots, sort_slot, 0)
+    lax.fori_loop(1, EARLY_STEPS, phase_step, 0)
+    raw_twin.wait()
+    lax.fori_loop(other * slots, other * slots + slots, sort_slot, 0)
     for c in range(chunks):
         for i in range(OVER_X):
-            x_stage[c, i] = pool[c, route_ref[base + i]]
+            x_stage[c, i] = pool[c, route_ref[i]]
         x_copy(c).start()
 
     lax.fori_loop(EARLY_STEPS, steps, phase_step, 0)
-    at = lax.broadcasted_iota(jnp.int32, (size, size), 0)
-    to = lax.broadcasted_iota(jnp.int32, (size, size), 1)
-    order[...] = jnp.where(at % quarter * RADIX + at // quarter == to, 1.0, 0.0).astype(BF16)
+    right_tables(half_ref, right_ref)
+    left_tables(half_ref, left_ref)
+    at = lax.broadcasted_iota(jnp.int32, (quarter, half), 0)
+    to = lax.broadcasted_iota(jnp.int32, (quarter, half), 1)
+    for k in range(RADIX):
+        for side in range(2):
+            raw[2 * k + side] = jnp.where(at * RADIX + k == to + side * half, 1.0, 0.0).astype(BF16)
 
     def pick_x(c, index):
-        mine = pool[c, jnp.minimum(index, 2 * slots - 1)]
+        mine = pool[c, jnp.clip(index, 0, 2 * slots - 1)]
         far = x_got[c][jnp.clip(index - 2 * slots, 0, OVER_X - 1)]
         return jnp.where(index < 2 * slots, mine, far)
 
-    def route(c):
-        x_copy(c).wait()
+    def route_y(c):
+        x_copy(c).wait_recv()
         for i in range(OVER_Y):
-            y_stage[c, i] = pick_x(c, route_ref[base + OVER_X + i])
+            y_stage[c, i] = pick_x(c, route_ref[OVER_X + i])
         y_copy(c).start()
-        y_copy(c).wait()
+
+    def route_z(c):
+        y_copy(c).wait_recv()
         for i in range(STARS_CHIP):
-            index = route_ref[base + OVER_X + OVER_Y + i]
+            index = route_ref[OVER_X + OVER_Y + i]
             far = y_got[c][jnp.clip(index - 2 * slots - OVER_X, 0, OVER_Y - 1)]
             near = pick_x(c, jnp.minimum(index, 2 * slots + OVER_X - 1))
-            z_stage[c, i] = jnp.where(index < 2 * slots + OVER_X, near, far)
-        for copy in z_copies(c):
-            copy.start()
-
-    for c in range(chunks // 2):
-        route(c)
+            raw[2 * RADIX + i, c * piece : (c + 1) * piece] = jnp.where(
+                index < 2 * slots + OVER_X, near, far
+            )
+        z_start(c)
 
     blocks = [slice(m * quarter, (m + 1) * quarter) for m in range(RADIX)]
     centre = 0.5 * (size - 1)
@@ -517,8 +597,7 @@
     tile = lanes * depth
 
     def forward_columns(step, carry):
-        for copy in turn_copies(step):
-            copy.wait()
+        turns_wait(step)
         rows = group_rows(step, depth, row_count, lanes)
         turns = jnp.concatenate([turns_out[r, :] for r in rows], 0)
         cosine, sine = turn_cos_sin(turns.astype(F32))
@@ -541,17 +620,17 @@
                 yi[rows[lane], blocks[k]] = made[lined, quarter:]
         return carry
 
-    lax.fori_loop(0, steps, forward_columns, 0)
-    for c in range(chunks // 2, chunks):
-        route(c)
-
     def focal(kind, carry):
         for part in range(parts):
-            for copy in z_copies(kind * parts + part):
-                copy.wait()
-        ct_turned[...] = lax.dot_general(
-            order[...], ct[kind], (((1,), (1,)), ((), ())), preferred_element_type=F32
-        )
+            z_local_copy(kind * parts + part).wait()
+            z_arrival(kind * parts + part).wait_recv()
+        for side in range(2):
+            cols = slice(side * half, (side + 1) * half)
+            order = jnp.concatenate([raw[2 * k + side] for k in range(RADIX)], 0)
+            turned = lax.dot_general(
+                order, ct[kind, :, cols], (((1,), (1,)), ((), ())), preferred_element_type=F32
+            )
+            ct_turned[...] = turned if side == 0 else ct_turned[...] + turned
         cols = pl.ds(pl.multiple_of(kind * quarter, quarter), quarter)
         mixed_real, mixed_imag = butterfly(
             [yr[b, cols].astype(F32) for b in blocks],
@@ -573,10 +652,24 @@
             xi[blocks[m], cols] = (spec_imag[m] * scale).astype(BF16)
         return carry
 
-    lax.fori_loop(0, RADIX, focal, 0)
-
-
-def focal_fields(cells, inverse, route, coef_table, feature_maps, cotangent, right, left, groups, lanes):
+    column_plan = {chunks // 4: (0, 3), 3 * chunks // 8: (3, 6), 5 * chunks // 8: (6, 8)}
+    focal_plan = {chunks - 2: 0, chunks - 1: 1}
+    for c in range(chunks):
+        route_y(c)
+        if c in column_plan:
+            first, last = column_plan[c]
+            lax.fori_loop(first * steps // 8, last * steps // 8, forward_columns, 0)
+        if c in focal_plan:
+            focal(focal_plan[c], 0)
+        route_z(c)
+    lax.fori_loop(len(focal_plan), RADIX, focal, 0)
+    sized = raw.at[pl.ds(0, len(places))]
+    send(sized, sized, z_send, z_recv.at[0], peers[0]).wait_send()
+    send(x_stage, x_stage, x_send, x_recv.at[0], {"star": over_x}).wait_send()
+    send(y_stage, y_stage, y_send, y_recv.at[0], {"star": over_y}).wait_send()
+
+
+def focal_fields(counts, cells, bands, coef_table, feature_maps, cotangent, halves, groups, lanes):
     map_count, row_count, size = feature_maps.shape
     slots = cotangent.shape[0]
     depth = row_count // TURN_STEPS
@@ -587,64 +680,68 @@
     smem = pl.BlockSpec(memory_space=pltpu.SMEM)
     vmem = pl.BlockSpec(memory_space=pltpu.VMEM)
     hbm = pl.BlockSpec(memory_space=pl.ANY)
-    square = jax.ShapeDtypeStruct((size, size), BF16)
-    others = 2 * lanes - 1
+    square = pltpu.VMEM((size, size), BF16)
     return pl.pallas_call(
         functools.partial(focal_kernel, groups, lanes),
-        out_shape=(square,) * 3,
-        in_specs=[smem, smem, smem, vmem, hbm, hbm, vmem, vmem],
-        out_specs=(vmem,) * 3,
+        out_shape=(square,) * 3 + (pltpu.VMEM((RADIX, half, half), BF16),),
+        in_specs=[pl.BlockSpec(memory_space=pltpu.HBM)] * 4 + [hbm, hbm, vmem],
+        out_specs=(vmem,) * 4,
         scratch_shapes=[
             pltpu.VMEM((RADIX, half, half), BF16),
-            pltpu.VMEM((RADIX, half, half), BF16),
-            pltpu.VMEM((2, map_count, depth, size), BF16),
+            pltpu.VMEM((depth // ROWS_STEP, map_count, ROWS_STEP, size), BF16),
             pltpu.VMEM((lanes, row_count, size), BF16),
             pltpu.VMEM((2 * slots, row_count, half), BF16),
             pltpu.VMEM((chunks, 2 * slots, piece, half), BF16),
             pltpu.VMEM((chunks, OVER_X, piece, half), BF16),
             pltpu.VMEM((chunks, OVER_Y, piece, half), BF16),
-            pltpu.VMEM((chunks, STARS_CHIP, piece, half), BF16),
             pltpu.VMEM((RADIX, quarter, size), BF16),
             pltpu.VMEM((size, quarter), F32),
-            pltpu.VMEM((size, size), BF16),
             pltpu.VMEM((lanes * ROWS_STEP, map_count * ROWS_STEP), BF16),
             pltpu.VMEM((size, size), BF16),
             pltpu.VMEM((size, size), BF16),
         ]
+        + [
+            pltpu.SMEM((OVER_X + OVER_Y + STARS_CHIP,), jnp.int32),
+            pltpu.SMEM(counts.shape, jnp.int32),
+            pltpu.SMEM(cells.shape, jnp.int32),
+            pltpu.SMEM(bands.shape, jnp.int32),
+            pltpu.VMEM(coef_table.shape, BF16),
+            dma((4,)),
+        ]
         + [pltpu.VMEM((OVER_X, piece, half), BF16)] * chunks
         + [pltpu.VMEM((OVER_Y, piece, half), BF16)] * chunks
         + [
-            dma((2,)),
+            dma((depth // ROWS_STEP,)),
             dma((TURN_STEPS,)),
-            dma((TURN_STEPS, lanes - 1)),
+            dma((TURN_STEPS,)),
             dma((TURN_STEPS, lanes - 1)),
             dma,
             dma,
             dma,
+            dma,
+            dma((chunks,)),
+            dma,
             dma((chunks,)),
             dma((chunks,)),
+            dma,
             dma((chunks,)),
-            dma((chunks,)),
-            dma((chunks,)),
-            dma((chunks, others)),
-            dma((chunks, others)),
         ],
         compiler_params=pltpu.CompilerParams(
-            collective_id=0, has_side_effects=True, vmem_limit_bytes=60 << 20
+            collective_id=0, has_side_effects=True, vmem_limit_bytes=K1_LIMIT << 20
         ),
         name="focal_fields",
-    )(cells, inverse, route, coef_table, feature_maps, cotangent, right, left)
+    )(counts, cells, bands, coef_table, feature_maps, cotangent, halves)
 
 
 def gradient_kernel(
-    groups, lanes, cell_ref, wave_ref, coef_ref, turns_ref, xr, xi, half_ref, maps_ref, grad_out, coef_out,
-    left, gathered, away, maps_buf, sums_buf, score, weights, row_part, star_part,
-    m_sem, o_sem, z_send, z_recv, p_send, p_recv, c_send, c_recv, sr_send, sr_recv, ss_send, ss_recv,
+    groups, lanes, count_ref, cells_ref, bands_ref, coef_ref, turns_ref, xr, xi, left, maps_ref,
+    grad_out, coef_out, cell_ref, gathered, away, maps_buf, score, weights, row_part, star_part,
+    m_sem, z_send, z_recv, p_send, p_recv, c_send, c_recv, sr_send, sr_recv, ss_send, ss_recv,
 ):
     row = lax.axis_index("row")
     me = lax.axis_index("star")
     steps = GATHER_STEPS
-    share = sums_buf.shape[1]
+    share = grad_out.shape[0]
     map_count, row_count, size = maps_ref.shape
     depth = row_count // steps
     parts = depth // ROWS_STEP
@@ -666,35 +763,13 @@
 
     for part in range(parts):
         fetch(0, part).start()
-    whole_tables(half_ref, left, 1)
+
+    slots = cells_ref.shape[1]
+    routes, cell_at, wave_at = star_plan(slots, count_ref, cells_ref, bands_ref)
+    wave = wave_at(me // 2, me % 2 * lanes + row, 2.0 * np.pi)
 
     def cell_of(group, d):
         return cell_ref[group * lanes + (row + lanes - d) % lanes]
-
-    at = lax.broadcasted_iota(jnp.int32, (total, coef_ref.shape[0]), 0)
-    to = lax.broadcasted_iota(jnp.int32, (total, coef_ref.shape[0]), 1)
-    wanted = jnp.zeros_like(at)
-    for group in range(groups):
-        for d in range(lanes):
-            wanted = jnp.where(at == group * lanes + d, cell_of(group, d), wanted)
-    hot = jnp.where(to == wanted, 1.0, 0.0).astype(BF16)
-    rows_of = jnp.dot(hot, coef_ref[...], preferred_element_type=F32).astype(BF16)
-    lines = share * ROWS_STEP
-    wide = total * ROWS_STEP
-    at = lax.broadcasted_iota(jnp.int32, (lines, map_count), 0)
-    to = lax.broadcasted_iota(jnp.int32, (lines, map_count), 1)
-    mine = jnp.where(to == me * share + at // ROWS_STEP, 1.0, 0.0).astype(BF16)
-    columns = lax.dot_general(
-        mine, rows_of, (((1,), (1,)), ((), ())), preferred_element_type=F32
-    ).astype(BF16)
-    at = lax.broadcasted_iota(jnp.int32, (total, wide), 0)
-    to = lax.broadcasted_iota(jnp.int32, (total, wide), 1)
-    repeat = jnp.where(to // ROWS_STEP == at, 1.0, 0.0).astype(BF16)
-    repeated = jnp.dot(columns, repeat, preferred_element_type=F32)
-    at = lax.broadcasted_iota(jnp.int32, (lines, wide), 0)
-    to = lax.broadcasted_iota(jnp.int32, (lines, wide), 1)
-    weights[...] = jnp.where(at % ROWS_STEP == to % ROWS_STEP, repeated, 0.0).astype(BF16)
-    score[...] = jnp.zeros_like(score)
 
     blocks = [slice(m * quarter, (m + 1) * quarter) for m in range(RADIX)]
     centre = 0.5 * (size - 1)
@@ -706,47 +781,30 @@
     def block(group, step, first=0, count=lanes):
         return gathered.at[group, pl.ds(first, count), rows_at(step)]
 
-    def z_copies(step):
-        return [
+    def z_start(step):
+        for d in range(1, lanes):
             send(
                 away.at[d - 1, rows_at(step)],
                 gathered.at[me, d, rows_at(step)],
-                z_send.at[step, d - 1],
-                z_recv.at[step, d - 1],
+                z_send,
+                z_recv.at[step],
                 row_peers[d - 1],
-            )
-            for d in range(1, lanes)
-        ]
+            ).start()
 
     def plane(step, way, part, peer):
-        return send(part, part, p_send.at[step, way], p_recv.at[step, way], peer)
-
-    def twin(step, way, part):
-        return send(part, part, c_send.at[step, way], c_recv.at[step, way], to_core)
-
-    def sides_own(step):
-        part = block(me, step, 0, 1)
-        return [plane(step, 0, part, to_across), plane(step, 1, part, to_along)]
-
-    def sides_rest(step):
-        part = block(me, step, 1, lanes - 1)
-        return [plane(step, 2, part, to_across), plane(step, 3, part, to_along)]
-
-    def corners(step):
-        return [
-            plane(step, 4, block(across, step, 0, half_lanes), to_along),
-            plane(step, 5, block(along, step, half_lanes, lanes - half_lanes), to_across),
-        ]
-
-    def twins(step, first=0, last=5):
-        parts = [
-            lambda: block(me, step, 0, 1),
-            lambda: block(me, step, 1, lanes - 1),
-            lambda: block(across, step),
-            lambda: block(along, step),
-            lambda: block(corner, step),
-        ]
-        return [twin(step, way, parts[way]()) for way in range(first, last)]
+        send(part, part, p_send, p_recv.at[step, way], peer).start()
+
+    def twin(step, part):
+        send(part, part, c_send, c_recv.at[step], to_core).start()
+
+    def sides(step, first, count):
+        part = block(me, step, first, count)
+        plane(step, 0, part, to_across)
+        plane(step, 0, part, to_along)
+        twin(step, part)
+
+    def arrived(part, sem):
+        send(part, part, p_send, sem, to_core).wait_recv()
 
     def columns_step(step):
         firsts = [(row + d) % lanes * row_count + step * depth for d in range(lanes)]
@@ -773,7 +831,6 @@
             part_real.append(made[:, :quarter])
             part_imag.append(made[:, quarter:])
         grad_real, grad_imag = butterfly(part_real, part_imag, 1)
-        wave = wave_ref[me * lanes + row]
         for m in range(RADIX):
             grad = real[:, blocks[m]] * grad_imag[m] - imag[:, blocks[m]] * grad_real[m]
             grad = (wave * grad).astype(BF16)
@@ -795,24 +852,12 @@
             def _():
                 fetch(step + 1, part).start()
 
-    def sums_out(step):
-        return pltpu.make_async_copy(
-            sums_buf.at[step % 2], grad_out.at[:, rows_at(step)], o_sem.at[step % 2]
-        )
-
     def sums_step(step):
-        @pl.when(step >= 2)
-        def _():
-            sums_out(step - 2).wait()
-
         for part in range(parts):
             rows = pl.ds(pl.multiple_of(step * depth + part * ROWS_STEP, ROWS_STEP), ROWS_STEP)
             grads = gathered[:, :, rows].reshape(wide, size)
             made = jnp.dot(weights[...], grads, preferred_element_type=F32)
-            sums_buf[step % 2, :, pl.ds(part * ROWS_STEP, ROWS_STEP)] = made.reshape(
-                share, ROWS_STEP, size
-            )
-        sums_out(step).start()
+            grad_out[:, rows] = made.reshape(share, ROWS_STEP, size)
 
     def row_copies():
         return [
@@ -860,40 +905,41 @@
         def _():
             body(tick - lag)
 
-    def compute(step):
+    def compute(step, carry):
         columns_step(step)
-        for copy in z_copies(step) + sides_own(step) + twins(step, 0, 1):
-            copy.start()
+        sides(step, 0, 1)
+        return carry
 
     def own_arrived(step):
-        for copy in z_copies(step):
-            copy.wait_recv()
-        for copy in sides_rest(step) + twins(step, 1, 2):
-            copy.start()
+        sized = away.at[:, rows_at(step)]
+        arrived(sized, z_recv.at[step])
+
+        @pl.when(step + Z_AHEAD < steps)
+        def _():
+            z_start(step + Z_AHEAD)
+
+        sides(step, 1, lanes - 1)
 
     def sides_arrived(step):
-        for copy in sides_own(step) + sides_rest(step):
-            copy.wait_recv()
-        for copy in corners(step) + twins(step, 2, 4):
-            copy.start()
+        arrived(gathered.at[pl.ds(0, 2), :, rows_at(step)], p_recv.at[step, 0])
+        plane(step, 1, block(across, step, 0, half_lanes), to_along)
+        plane(step, 1, block(along, step, half_lanes, lanes - half_lanes), to_across)
+        twin(step, block(across, step))
+        twin(step, block(along, step))
 
     def corners_arrived(step):
-        for copy in corners(step):
-            copy.wait_recv()
-        for copy in twins(step, 4):
-            copy.start()
+        arrived(gathered.at[pl.ds(0, 1), :, rows_at(step)], p_recv.at[step, 1])
+        twin(step, block(corner, step))
 
     def all_arrived(step):
-        for copy in twins(step):
-            copy.wait_recv()
+        arrived(gathered.at[pl.ds(0, groups // 2), :, rows_at(step)], c_recv.at[step])
         sums_step(step)
 
     def tick_body(tick, carry):
-        between(tick, 0, compute)
-        between(tick, 1, own_arrived)
-        between(tick, 2, sides_arrived)
-        between(tick, 3, corners_arrived)
-        between(tick, 1, score_step)
+        between(tick, 0, own_arrived)
+        between(tick, SIDES_LAG, sides_arrived)
+        between(tick, SIDES_LAG + CORNERS_LAG, corners_arrived)
+        between(tick, 0, score_step)
 
         @pl.when(tick == steps)
         def _():
@@ -903,28 +949,56 @@
         def _():
             scores_stars()
 
-        @pl.when(tick == steps + 2)
-        def _():
-            scores_end()
-
-        between(tick, 4, all_arrived)
+        between(tick, SIDES_LAG + CORNERS_LAG + 1, all_arrived)
         return carry
 
-    lax.fori_loop(0, steps + 4, tick_body, 0)
-
-    def drain(step, carry):
-        for copy in (
-            z_copies(step) + sides_own(step) + sides_rest(step) + corners(step) + twins(step)
-        ):
-            copy.wait_send()
+    columns_step(0)
+    greeted(row_peers + star_peers)
+    z_start(0)
+    sides(0, 0, 1)
+    for step in range(1, Z_AHEAD):
+        compute(step, 0)
+        z_start(step)
+    lax.fori_loop(Z_AHEAD, steps, compute, 0)
+    def cell_fill(chip, carry):
+        for place in range(STARS_CHIP):
+            cell_ref[chip * STARS_CHIP + place] = cell_at(chip, place)
         return carry
 
-    lax.fori_loop(0, steps, drain, 0)
-    for step in range(steps - 2, steps):
-        sums_out(step).wait()
-
-
-def gradient_sums(cells, wave, coef_table, turns, spec_real, spec_imag, halves, feature_maps, groups, lanes):
+    lax.fori_loop(0, total // STARS_CHIP, cell_fill, 0)
+    at = lax.broadcasted_iota(jnp.int32, (total, coef_ref.shape[0]), 0)
+    to = lax.broadcasted_iota(jnp.int32, (total, coef_ref.shape[0]), 1)
+    wanted = jnp.zeros_like(at)
+    for group in range(groups):
+        for d in range(lanes):
+            wanted = jnp.where(at == group * lanes + d, cell_of(group, d), wanted)
+    hot = jnp.where(to == wanted, 1.0, 0.0).astype(BF16)
+    rows_of = jnp.dot(hot, coef_ref[...], preferred_element_type=F32).astype(BF16)
+    lines = share * ROWS_STEP
+    wide = total * ROWS_STEP
+    at = lax.broadcasted_iota(jnp.int32, (lines, map_count), 0)
+    to = lax.broadcasted_iota(jnp.int32, (lines, map_count), 1)
+    mine = jnp.where(to == me * share + at // ROWS_STEP, 1.0, 0.0).astype(BF16)
+    columns = lax.dot_general(
+        mine, rows_of, (((1,), (1,)), ((), ())), preferred_element_type=F32
+    ).astype(BF16)
+    at = lax.broadcasted_iota(jnp.int32, (total, wide), 0)
+    to = lax.broadcasted_iota(jnp.int32, (total, wide), 1)
+    repeat = jnp.where(to // ROWS_STEP == at, 1.0, 0.0).astype(BF16)
+    repeated = jnp.dot(columns, repeat, preferred_element_type=F32)
+    at = lax.broadcasted_iota(jnp.int32, (lines, wide), 0)
+    to = lax.broadcasted_iota(jnp.int32, (lines, wide), 1)
+    weights[...] = jnp.where(at % ROWS_STEP == to % ROWS_STEP, repeated, 0.0).astype(BF16)
+    score[...] = jnp.zeros_like(score)
+    lax.fori_loop(0, steps + SIDES_LAG + CORNERS_LAG + 1, tick_body, 0)
+    scores_end()
+    send(away, away, z_send, z_recv.at[0], to_core).wait_send()
+    three, four = gathered.at[pl.ds(0, 3)], gathered.at[pl.ds(0, groups // 2)]
+    send(three, three, p_send, z_recv.at[0], to_core).wait_send()
+    send(four, four, c_send, z_recv.at[0], to_core).wait_send()
+
+
+def gradient_sums(counts, cells, bands, coef_table, turns, spec_real, spec_imag, left, feature_maps, groups, lanes):
     map_count, row_count, size = feature_maps.shape
     cell_count = coef_table.shape[0]
     share = map_count // groups
@@ -933,57 +1007,54 @@
     smem = pl.BlockSpec(memory_space=pltpu.SMEM)
     vmem = pl.BlockSpec(memory_space=pltpu.VMEM)
     hbm = pl.BlockSpec(memory_space=pl.ANY)
-    half = size // 2
     padded = -(-cell_count // 128) * 128
     return pl.pallas_call(
         functools.partial(gradient_kernel, groups, lanes),
         out_shape=(
-            jax.ShapeDtypeStruct((share, row_count, size), F32),
+            pltpu.VMEM((share, row_count, size), F32),
             jax.ShapeDtypeStruct((cell_count, map_count), F32),
         ),
-        in_specs=[smem, smem, vmem, vmem, vmem, vmem, vmem, hbm],
-        out_specs=(hbm, vmem),
+        in_specs=[smem, smem, smem, vmem, vmem, vmem, vmem, vmem, hbm],
+        out_specs=(vmem, vmem),
         scratch_shapes=[
-            pltpu.VMEM((RADIX, half, half), BF16),
+            pltpu.SMEM((groups * lanes,), jnp.int32),
             pltpu.VMEM((groups, lanes, row_count, size), BF16),
             pltpu.VMEM((lanes - 1, row_count, size), BF16),
             pltpu.VMEM((depth // ROWS_STEP, map_count, ROWS_STEP, size), BF16),
-            pltpu.VMEM((2, share, depth, size), F32),
             pltpu.VMEM((map_count * ROWS_STEP, lanes * ROWS_STEP), F32),
             pltpu.VMEM((share * ROWS_STEP, groups * lanes * ROWS_STEP), BF16),
             pltpu.VMEM((lanes, map_count, padded), F32),
             pltpu.VMEM((groups, map_count, padded), F32),
             dma((depth // ROWS_STEP,)),
-            dma((2,)),
-            dma((GATHER_STEPS, lanes - 1)),
-            dma((GATHER_STEPS, lanes - 1)),
-            dma((GATHER_STEPS, 6)),
-            dma((GATHER_STEPS, 6)),
-            dma((GATHER_STEPS, 5)),
-            dma((GATHER_STEPS, 5)),
+            dma,
+            dma((GATHER_STEPS,)),
+            dma,
+            dma((GATHER_STEPS, 2)),
+            dma,
+            dma((GATHER_STEPS,)),
             dma((lanes - 1,)),
             dma((lanes - 1,)),
             dma((groups - 1,)),
             dma((groups - 1,)),
         ],
         compiler_params=pltpu.CompilerParams(
-            collective_id=1, has_side_effects=True, vmem_limit_bytes=60 << 20
+            collective_id=1, has_side_effects=True, vmem_limit_bytes=K2_LIMIT << 20
         ),
         name="gradient_sums",
-    )(cells, wave, coef_table, turns, spec_real, spec_imag, halves, feature_maps)
+    )(counts, cells, bands, coef_table, turns, spec_real, spec_imag, left, feature_maps)
 
 
 def star_devices(feature_maps, coef_table, star_counts, star_cells, star_bands, psf_cotangent):
     groups = lax.axis_size("star")
     lanes = lax.axis_size("row")
     size = feature_maps.shape[2]
-    cells, inverse, wave, route = plan(star_counts, star_cells, star_bands)
-    right, left = half_tables(size)
-    turns, spec_real, spec_imag = focal_fields(
-        cells, inverse, route, coef_table, feature_maps, psf_cotangent, right, left, groups, lanes
+    halves = half_tables(size)
+    turns, spec_real, spec_imag, left = focal_fields(
+        star_counts, star_cells, star_bands, coef_table, feature_maps, psf_cotangent, halves, groups, lanes
     )
     return gradient_sums(
-        cells, wave, coef_table, turns, spec_real, spec_imag, left, feature_maps, groups, lanes
+        star_counts, star_cells, star_bands, coef_table, turns, spec_real, spec_imag, left, feature_maps,
+        groups, lanes,
     )
 
 

time: 212 us -> 181 us (0.85)
  Pallas kernels: 201 us -> 176 us
  local copies, waits for them, and re-layouts: 9.07 us -> 4.03 us
    pallas_call x1, Pallas kernels: 91.7 us -> 79 us  [gradient_sums(): pl.pallas_call(functools.partial(gradient_kernel, groups, lanes), out_sha...]
    pallas_call x1, Pallas kernels: 107 us -> 96.6 us  [focal_fields(): pl.pallas_call(functools.partial(focal_kernel, groups, lanes), out_shape=...]
    unnamed x4 -> x10, local copies, waits for them, and re-layouts: 9.07 us -> 4.03 us
    pallas_call x1 -> x0, Pallas kernels: 2.89 us -> none  [plan(): pl.pallas_call(functools.partial(plan_kernel, slots), out_shape=(jax.Shap...]
where the time goes in v3:
time: 181 us; the launch traced here: 180 us
  Pallas kernels  176 us (97%)
  local copies, waits for them, and re-layouts  4.03 us (2%)
    pallas_call x1, Pallas kernels, focal_fields(): pl.pallas_call(functools.partial(focal_kernel, groups, lanes), out_shape=...  96.6 us
    pallas_call x1, Pallas kernels, gradient_sums(): pl.pallas_call(functools.partial(gradient_kernel, groups, lanes), out_sha...  79 us
    unnamed x10, local copies, waits for them, and re-layouts  4.03 us

profile of v3, /device:TPU:27, one launch (start us, length us, event | category | flops | bytes accessed | tf_op | source)
XLA Modules:
  0.0 180.3 jit_solution(8336380655170132304)
XLA Ops:
  0.6 0.0 copy-start.2
  0.6 0.0 copy-start.1
  0.7 0.0 copy-start.3
  0.7 0.0 copy-start
  0.7 96.6 %focal_fields.1 = (bf16[1024,1024]{1,0:T(8,128)(2,1)S(1)}, bf16[1024,1024]{1,0:T(8,128)(2,1)S(1)}, bf16[1024,1024]{1,0:T(8,128)(2,1)S(1)}, bf16[4,512,512]{2,1,0:T(8,128)(2,1)S(1)}) custom-call(s32[8]{0:T(128)} %count_ref.1, s32[8,12]{1,0:T(8,128)} %cells_ref.1, s32[8,12]{1,0:T(8,128)} %bands_ref.1, bf16[64,64]{1,0:T(8,128)(2,1)} %coef_ref.1, ...), custom_call_target="tpu_custom_call" | custom-call | tf_op jit(solution)/shard_map/focal_fields/pallas_call | solution.py:684
  97.2 0.0 copy-done.2
  97.3 0.0 copy-done.1
  97.3 0.0 copy-done.3
  97.3 0.0 copy-done
  97.3 79.0 %gradient_sums.1 = (f32[8,256,1024]{2,1,0:T(8,128)S(1)}, f32[64,64]{1,0:T(8,128)S(1)}) custom-call(s32[8]{0:T(128)S(1)} %copy-done.3, s32[8,12]{1,0:T(8,128)S(1)} %copy-done.1, s32[8,12]{1,0:T(8,128)S(1)} %copy-done.2, bf16[64,64]{1,0:T(8,128)(2,1)S(1)} %copy-done, bf16[1024,1024]{1,0:T(8,128)(2,1)S(1)} %get-tuple-element.6.turns_ref, ...), custom_call_target="tpu_custom_call" | custom-call | tf_op jit(solution)/shard_map/gradient_sums/pallas_call | solution.py:1011
  176.3 3.4 %copy.11 = f32[8,256,1024]{2,1,0:T(8,128)} copy(f32[8,256,1024]{2,1,0:T(8,128)S(1)} %get-tuple-element.10) | data formatting | bytes 16777216
  179.7 0.6 copy.12
Async XLA Ops:
  0.6 96.6 %copy-start.2 = (s32[8,12]{1,0:T(8,128)S(1)}, s32[8,12]{1,0:T(8,128)}, u32[]{:S(2)}) copy-start(s32[8,12]{1,0:T(8,128)} %bands_ref.1) | copy-start | bytes 1156
  0.6 96.6 %copy-start.1 = (s32[8,12]{1,0:T(8,128)S(1)}, s32[8,12]{1,0:T(8,128)}, u32[]{:S(2)}) copy-start(s32[8,12]{1,0:T(8,128)} %cells_ref.1) | copy-start | bytes 1156
  0.7 96.6 %copy-start.3 = (s32[8]{0:T(128)S(1)}, s32[8]{0:T(128)}, u32[]{:S(2)}) copy-start(s32[8]{0:T(128)} %count_ref.1) | copy-start | bytes 100
  0.7 96.6 %copy-start = (bf16[64,64]{1,0:T(8,128)(2,1)S(1)}, bf16[64,64]{1,0:T(8,128)(2,1)}, u32[]{:S(2)}) copy-start(bf16[64,64]{1,0:T(8,128)(2,1)} %coef_ref.1) | copy-start | bytes 24580

commit v4 on v3

--- a/solution.py
+++ b/solution.py
@@ -378,17 +378,23 @@
     greet(peers_all)
 
     slot_range = pl.ds(core * slots, slots)
+    some = slots // 2
     other = 1 - core
     raw_own = pltpu.make_async_copy(
         cot_ref.at[:, :, pl.ds(pl.multiple_of(core * half, half), half)], raw.at[slot_range], r_local
     )
-    raw_twin = send(
-        cot_ref.at[:, :, pl.ds(pl.multiple_of(other * half, half), half)],
-        raw.at[slot_range],
-        r_send,
-        r_recv,
-        {"star": twin},
-    )
+    raw_twin = [
+        send(
+            cot_ref.at[
+                pl.ds(part * some, some), :, pl.ds(pl.multiple_of(other * half, half), half)
+            ],
+            raw.at[pl.ds(core * slots + part * some, some)],
+            r_send.at[part],
+            r_recv.at[part],
+            {"star": twin},
+        )
+        for part in range(2)
+    ]
     raw_own.start()
 
     def fetch(step, part):
@@ -397,6 +403,9 @@
 
     for part in range(depth // ROWS_STEP):
         fetch(0, part).start()
+    greeted(peers_all)
+    for copy in raw_twin:
+        copy.start()
     for copy in small:
         copy.wait()
     routes, cell_at, wave_at = star_plan(slots, count_ref, cells_ref, bands_ref)
@@ -547,14 +556,14 @@
     at = lax.broadcasted_iota(jnp.int32, (row_count, row_count), 0)
     to = lax.broadcasted_iota(jnp.int32, (row_count, row_count), 1)
     sort = jnp.where(at % tall * RADIX + at // tall == to, 1.0, 0.0).astype(BF16)
-    greeted(peers_all)
-    raw_twin.start()
     turns_start(0)
     raw_own.wait()
     lax.fori_loop(core * slots, core * slots + slots, sort_slot, 0)
     lax.fori_loop(1, EARLY_STEPS, phase_step, 0)
-    raw_twin.wait()
-    lax.fori_loop(other * slots, other * slots + slots, sort_slot, 0)
+    for part in range(2):
+        raw_twin[part].wait()
+        begin = other * slots + part * some
+        lax.fori_loop(begin, begin + some, sort_slot, 0)
     for c in range(chunks):
         for i in range(OVER_X):
             x_stage[c, i] = pool[c, route_ref[i]]
@@ -716,8 +725,8 @@
             dma((TURN_STEPS,)),
             dma((TURN_STEPS, lanes - 1)),
             dma,
-            dma,
-            dma,
+            dma((2,)),
+            dma((2,)),
             dma,
             dma((chunks,)),
             dma,

time: 181 us -> 179 us (0.989)
  no operation moved by 1% of the time
where the time goes in v4:
time: 179 us
  Pallas kernels  175 us (98%)
  local copies, waits for them, and re-layouts  4.03 us (2%)
    pallas_call x1, Pallas kernels, focal_fields(): pl.pallas_call(functools.partial(focal_kernel, groups, lanes), out_shape=...  95.5 us
    pallas_call x1, Pallas kernels, gradient_sums(): pl.pallas_call(functools.partial(gradient_kernel, groups, lanes), out_sha...  79 us
    unnamed x10, local copies, waits for them, and re-layouts  4.03 us

profile of v4, /device:TPU:27, one launch (start us, length us, event | category | flops | bytes accessed | tf_op | source)
XLA Modules:
  0.0 179.3 jit_solution(1649152692680979372)
XLA Ops:
  0.6 0.0 copy-start.2
  0.6 0.0 copy-start.1
  0.7 0.0 copy-start.3
  0.7 0.0 copy-start
  0.7 95.5 %focal_fields.1 = (bf16[1024,1024]{1,0:T(8,128)(2,1)S(1)}, bf16[1024,1024]{1,0:T(8,128)(2,1)S(1)}, bf16[1024,1024]{1,0:T(8,128)(2,1)S(1)}, bf16[4,512,512]{2,1,0:T(8,128)(2,1)S(1)}) custom-call(s32[8]{0:T(128)} %count_ref.1, s32[8,12]{1,0:T(8,128)} %cells_ref.1, s32[8,12]{1,0:T(8,128)} %bands_ref.1, bf16[64,64]{1,0:T(8,128)(2,1)} %coef_ref.1, ...), custom_call_target="tpu_custom_call" | custom-call | tf_op jit(solution)/shard_map/focal_fields/pallas_call | solution.py:693
  96.2 0.0 copy-done.2
  96.2 0.0 copy-done.1
  96.2 0.0 copy-done.3
  96.2 0.0 copy-done
  96.2 79.0 %gradient_sums.1 = (f32[8,256,1024]{2,1,0:T(8,128)S(1)}, f32[64,64]{1,0:T(8,128)S(1)}) custom-call(s32[8]{0:T(128)S(1)} %copy-done.3, s32[8,12]{1,0:T(8,128)S(1)} %copy-done.1, s32[8,12]{1,0:T(8,128)S(1)} %copy-done.2, bf16[64,64]{1,0:T(8,128)(2,1)S(1)} %copy-done, bf16[1024,1024]{1,0:T(8,128)(2,1)S(1)} %get-tuple-element.6.turns_ref, ...), custom_call_target="tpu_custom_call" | custom-call | tf_op jit(solution)/shard_map/gradient_sums/pallas_call | solution.py:1020
  175.3 3.4 %copy.11 = f32[8,256,1024]{2,1,0:T(8,128)} copy(f32[8,256,1024]{2,1,0:T(8,128)S(1)} %get-tuple-element.10) | data formatting | bytes 16777216
  178.7 0.6 copy.12
Async XLA Ops:
  0.6 95.6 %copy-start.2 = (s32[8,12]{1,0:T(8,128)S(1)}, s32[8,12]{1,0:T(8,128)}, u32[]{:S(2)}) copy-start(s32[8,12]{1,0:T(8,128)} %bands_ref.1) | copy-start | bytes 1156
  0.6 95.6 %copy-start.1 = (s32[8,12]{1,0:T(8,128)S(1)}, s32[8,12]{1,0:T(8,128)}, u32[]{:S(2)}) copy-start(s32[8,12]{1,0:T(8,128)} %cells_ref.1) | copy-start | bytes 1156
  0.7 95.6 %copy-start.3 = (s32[8]{0:T(128)S(1)}, s32[8]{0:T(128)}, u32[]{:S(2)}) copy-start(s32[8]{0:T(128)} %count_ref.1) | copy-start | bytes 100
  0.7 95.6 %copy-start = (bf16[64,64]{1,0:T(8,128)(2,1)S(1)}, bf16[64,64]{1,0:T(8,128)(2,1)}, u32[]{:S(2)}) copy-start(bf16[64,64]{1,0:T(8,128)(2,1)} %coef_ref.1) | copy-start | bytes 24580

commit v5 on v4

--- a/solution.py
+++ b/solution.py
@@ -14,7 +14,7 @@
 RADIX = 4
 ROWS_STEP = 16
 TURN_STEPS = 8
-EARLY_STEPS = 2
+EARLY_STEPS = 3
 ROUTE_CHUNKS = 8
 GATHER_STEPS = 8
 Z_AHEAD = 2

time: 179 us -> 179 us (level)
  no operation moved by 1% of the time
where the time goes in v5:
time: 179 us
  Pallas kernels  174 us (97%)
  local copies, waits for them, and re-layouts  4.03 us (2%)
    pallas_call x1, Pallas kernels, focal_fields(): pl.pallas_call(functools.partial(focal_kernel, groups, lanes), out_shape=...  95.5 us
    pallas_call x1, Pallas kernels, gradient_sums(): pl.pallas_call(functools.partial(gradient_kernel, groups, lanes), out_sha...  79 us
    unnamed x10, local copies, waits for them, and re-layouts  4.03 us

profile of v5, /device:TPU:27, one launch (start us, length us, event | category | flops | bytes accessed | tf_op | source)
XLA Modules:
  0.0 179.2 jit_solution(12541385790146478795)
XLA Ops:
  0.6 0.0 copy-start.2
  0.6 0.0 copy-start.1
  0.7 0.0 copy-start.3
  0.7 0.0 copy-start
  0.7 95.5 %focal_fields.1 = (bf16[1024,1024]{1,0:T(8,128)(2,1)S(1)}, bf16[1024,1024]{1,0:T(8,128)(2,1)S(1)}, bf16[1024,1024]{1,0:T(8,128)(2,1)S(1)}, bf16[4,512,512]{2,1,0:T(8,128)(2,1)S(1)}) custom-call(s32[8]{0:T(128)} %count_ref.1, s32[8,12]{1,0:T(8,128)} %cells_ref.1, s32[8,12]{1,0:T(8,128)} %bands_ref.1, bf16[64,64]{1,0:T(8,128)(2,1)} %coef_ref.1, ...), custom_call_target="tpu_custom_call" | custom-call | tf_op jit(solution)/shard_map/focal_fields/pallas_call | solution.py:693
  96.2 0.0 copy-done.2
  96.2 0.0 copy-done.1
  96.2 0.0 copy-done.3
  96.2 0.0 copy-done
  96.2 79.0 %gradient_sums.1 = (f32[8,256,1024]{2,1,0:T(8,128)S(1)}, f32[64,64]{1,0:T(8,128)S(1)}) custom-call(s32[8]{0:T(128)S(1)} %copy-done.3, s32[8,12]{1,0:T(8,128)S(1)} %copy-done.1, s32[8,12]{1,0:T(8,128)S(1)} %copy-done.2, bf16[64,64]{1,0:T(8,128)(2,1)S(1)} %copy-done, bf16[1024,1024]{1,0:T(8,128)(2,1)S(1)} %get-tuple-element.6.turns_ref, ...), custom_call_target="tpu_custom_call" | custom-call | tf_op jit(solution)/shard_map/gradient_sums/pallas_call | solution.py:1020
  175.2 3.4 %copy.11 = f32[8,256,1024]{2,1,0:T(8,128)} copy(f32[8,256,1024]{2,1,0:T(8,128)S(1)} %get-tuple-element.10) | data formatting | bytes 16777216
  178.6 0.6 copy.12
Async XLA Ops:
  0.6 95.6 %copy-start.2 = (s32[8,12]{1,0:T(8,128)S(1)}, s32[8,12]{1,0:T(8,128)}, u32[]{:S(2)}) copy-start(s32[8,12]{1,0:T(8,128)} %bands_ref.1) | copy-start | bytes 1156
  0.6 95.6 %copy-start.1 = (s32[8,12]{1,0:T(8,128)S(1)}, s32[8,12]{1,0:T(8,128)}, u32[]{:S(2)}) copy-start(s32[8,12]{1,0:T(8,128)} %cells_ref.1) | copy-start | bytes 1156
  0.7 95.6 %copy-start.3 = (s32[8]{0:T(128)S(1)}, s32[8]{0:T(128)}, u32[]{:S(2)}) copy-start(s32[8]{0:T(128)} %count_ref.1) | copy-start | bytes 100
  0.7 95.6 %copy-start = (bf16[64,64]{1,0:T(8,128)(2,1)S(1)}, bf16[64,64]{1,0:T(8,128)(2,1)}, u32[]{:S(2)}) copy-start(bf16[64,64]{1,0:T(8,128)(2,1)} %coef_ref.1) | copy-start | bytes 24580
